TPU v7x, 128 devices: a whole 4x4x4 slice. The times are simulated.
128 devices in a mesh: dp: 8 (over z, x_hi), tensor: 16 (over y, x_lo, core).
Axes of the slice: x: 4 (x_hi: 2, x_lo: 2; x = x_hi * 2 + x_lo), y: 4, z: 4, core: 2. Of those that a mesh axis runs over, the one named last changes fastest.
Arguments:
- tokens: bfloat16 [4096, 8192], P('dp', 'tensor'), may hold values from -6 to 6
- frozen: bfloat16 [8192, 8192], P('tensor'), may hold values from -0.0625 to 0.0625
- local_param: float32 [64, 128, 128], P('tensor'), may hold values from -0.2 to 0.2
- cross_param: float32 [4, 64, 128, 128], P(None, 'tensor'), may hold values from -0.2 to 0.2
- out_grad: bfloat16 [4096, 8192], P('dp', 'tensor'), may hold values from -0.09375 to 0.09375
Outputs:
- output: float32 [4096, 8192], P('dp', 'tensor')
- local_grad: float32 [64, 128, 128], P('tensor')
- cross_grad: float32 [4, 64, 128, 128], P(None, 'tensor')
All inputs are finite; a program needn't handle non-finite values.
Results may differ from a plain program's by a relative error of at most 0.0029.
Values may be sent and summed in bfloat16 or wider, within the bound.
A program may use at most 192 MiB of HBM per device.

v0:
```python
import jax
import jax.numpy as jnp
from jax import lax
from jax.sharding import PartitionSpec as P


def from_partner(shard, axis, stride):
    return lax.ppermute(shard, axis, [(i, i ^ 1 << stride) for i in range(lax.axis_size(axis))])


def cayley_block(param):
    highest = lax.Precision.HIGHEST
    skew = param - param.T
    identity = jnp.eye(param.shape[0], dtype=param.dtype)
    one_minus = identity - skew
    spd_matrix = identity - jnp.dot(skew, skew, precision=highest)
    numerator = jnp.dot(one_minus, one_minus, precision=highest)
    chol_factor = jnp.linalg.cholesky(spd_matrix)
    return jax.scipy.linalg.cho_solve((chol_factor, True), numerator.T).T


def cayley_many(params):
    return jax.vmap(cayley_block)(params)


def cayley_pull(param, matrix_grad):
    unused, pullback = jax.vjp(cayley_many, param)
    return pullback(matrix_grad)[0]


def split_halves(state, upper_side, blocks_dev, half_block):
    halves = state.reshape(state.shape[0], 2, blocks_dev, half_block)
    own_part = jnp.where(upper_side, halves[:, 1], halves[:, 0])
    other_part = jnp.where(upper_side, halves[:, 0], halves[:, 1])
    return (own_part, other_part)


def join_pair(own_part, received, upper_side):
    low_half = jnp.where(upper_side, received, own_part)
    high_half = jnp.where(upper_side, own_part, received)
    return jnp.concatenate([low_half, high_half], axis=-1)


def split_pair(vector, upper_side, half_block):
    low_half = vector[..., :half_block]
    high_half = vector[..., half_block:]
    keep_part = jnp.where(upper_side, high_half, low_half)
    give_part = jnp.where(upper_side, low_half, high_half)
    return (keep_part, give_part)


def merge_halves(keep_part, returned, upper_side):
    first_half = jnp.where(upper_side, returned, keep_part)
    second_half = jnp.where(upper_side, keep_part, returned)
    return jnp.stack([first_half, second_half], axis=1).reshape(keep_part.shape[0], -1)


def sum_data(value):
    return lax.psum(value, "dp")


def body(tokens, frozen, local_param, cross_param, out_grad):
    highest = lax.Precision.HIGHEST
    token_count, rows_dev = tokens.shape
    block = local_param.shape[-1]
    half_block = block // 2
    blocks_dev = local_param.shape[0]
    levels = lax.axis_size("tensor").bit_length() - 1
    position = lax.axis_index("tensor")
    local_rot = cayley_many(local_param)
    cross_rot = [cayley_many(cross_param[level_idx]) for level_idx in range(levels)]
    inputs = tokens.astype(jnp.float32).reshape(token_count, blocks_dev, block)
    state = jnp.einsum("tci,cij->tcj", inputs, local_rot, precision=highest).reshape(
        token_count, rows_dev
    )
    saved = []
    for level_idx in range(levels):
        upper_side = position >> level_idx & 1 == 1
        own_part, other_part = split_halves(state, upper_side, blocks_dev, half_block)
        received = from_partner(other_part, "tensor", level_idx)
        vector = join_pair(own_part, received, upper_side)
        mixed = jnp.einsum("tci,cij->tcj", vector, cross_rot[level_idx], precision=highest)
        keep_part, give_part = split_pair(mixed, upper_side, half_block)
        returned = from_partner(give_part, "tensor", level_idx)
        state = merge_halves(keep_part, returned, upper_side)
        saved.append(vector)
    rounded = state.astype(jnp.bfloat16)
    partial_out = jnp.dot(rounded, frozen, preferred_element_type=jnp.float32)
    output = lax.psum_scatter(partial_out, "tensor", scatter_dimension=1, tiled=True)
    grad_state = lax.dot_general(
        lax.all_gather(out_grad, "tensor", axis=1, tiled=True),
        frozen,
        (((1,), (1,)), ((), ())),
        preferred_element_type=jnp.float32,
    )
    cross_grads = [None] * levels
    for level_idx in reversed(range(levels)):
        upper_side = position >> level_idx & 1 == 1
        own_part, other_part = split_halves(grad_state, upper_side, blocks_dev, half_block)
        received = from_partner(other_part, "tensor", level_idx)
        grad_vector = join_pair(own_part, received, upper_side)
        matrix_grad = jnp.einsum("tci,tcj->cij", saved[level_idx], grad_vector, precision=highest)
        back_vector = jnp.einsum(
            "tcj,cij->tci", grad_vector, cross_rot[level_idx], precision=highest
        )
        keep_part, give_part = split_pair(back_vector, upper_side, half_block)
        returned = from_partner(give_part, "tensor", level_idx)
        grad_state = merge_halves(keep_part, returned, upper_side)
        param_grad = cayley_pull(cross_param[level_idx], matrix_grad)
        param_grad = sum_data(param_grad)
        cross_grads[level_idx] = param_grad
    grad_blocks = grad_state.reshape(token_count, blocks_dev, block)
    local_matrix = jnp.einsum("tci,tcj->cij", inputs, grad_blocks, precision=highest)
    local_grad = cayley_pull(local_param, local_matrix)
    local_grad = sum_data(local_grad)
    cross_grad = jnp.stack(cross_grads)
    return (output, local_grad, cross_grad)


def solution(mesh):
    in_specs = (
        P("dp", "tensor"),
        P("tensor", None),
        P("tensor", None, None),
        P(None, "tensor", None, None),
        P("dp", "tensor"),
    )
    out_specs = (P("dp", "tensor"), P("tensor", None, None), P(None, "tensor", None, None))
    return jax.shard_map(body, mesh=mesh, in_specs=in_specs, out_specs=out_specs, check_vma=False)
```

profile of v0, /device:TPU:6, one launch (start us, length us, event | category | flops | bytes accessed | tf_op | source)
XLA Modules:
  0.0 1782.9 jit_solution(9196138787854236795)
XLA Ops:
  24.4 48.0 %custom-call.110 = f32[4,128,128]{2,1,0:T(8,128)} custom-call(f32[4,128,128]{2,1,0:T(8,128)S(1)} %copy.622), custom_call_target="Cholesky" | custom-call | tf_op jit(solution)/shard_map/vmap(jit(cholesky))/cholesky/custom-call.1 | solution.py:18
  73.5 47.5 %custom-call.101 = f32[4,128,128]{2,1,0:T(8,128)} custom-call(f32[4,128,128]{2,1,0:T(8,128)S(1)} %copy.595), custom_call_target="Cholesky" | custom-call | tf_op jit(solution)/shard_map/vmap(jit(cholesky))/cholesky/custom-call.1 | solution.py:18
  122.1 47.5 %custom-call.104 = f32[4,128,128]{2,1,0:T(8,128)} custom-call(f32[4,128,128]{2,1,0:T(8,128)S(1)} %copy.604), custom_call_target="Cholesky" | custom-call | tf_op jit(solution)/shard_map/vmap(jit(cholesky))/cholesky/custom-call.1 | solution.py:18
  170.7 47.7 %custom-call.107 = f32[4,128,128]{2,1,0:T(8,128)} custom-call(f32[4,128,128]{2,1,0:T(8,128)S(1)} %copy.613), custom_call_target="Cholesky" | custom-call | tf_op jit(solution)/shard_map/vmap(jit(cholesky))/cholesky/custom-call.1 | solution.py:18
  219.5 47.6 %custom-call.98 = f32[4,128,128]{2,1,0:T(8,128)} custom-call(f32[4,128,128]{2,1,0:T(8,128)S(1)} %copy.586), custom_call_target="Cholesky" | custom-call | tf_op jit(solution)/shard_map/vmap(jit(cholesky))/cholesky/custom-call.1 | solution.py:18
  267.2 46.9 %custom-call.113 = f32[4,128,128]{2,1,0:T(8,128)S(1)} custom-call(f32[4,128,128]{2,1,0:T(8,128)S(1)} %fusion.150), custom_call_target="Cholesky" | custom-call | tf_op jit(solution)/shard_map/jvp(vmap(jit(cholesky)))/cholesky/custom-call.1 | solution.py:18
  319.3 47.9 %custom-call.131 = f32[4,128,128]{2,1,0:T(8,128)S(1)} custom-call(f32[4,128,128]{2,1,0:T(8,128)} %get-tuple-element.209), custom_call_target="Cholesky" | custom-call | tf_op jit(solution)/shard_map/jvp(vmap(jit(cholesky)))/cholesky/custom-call.1 | solution.py:18
  367.2 46.9 %custom-call.122 = f32[4,128,128]{2,1,0:T(8,128)S(1)} custom-call(f32[4,128,128]{2,1,0:T(8,128)S(1)} %get-tuple-element.210), custom_call_target="Cholesky" | custom-call | tf_op jit(solution)/shard_map/jvp(vmap(jit(cholesky)))/cholesky/custom-call.1 | solution.py:18
  417.1 46.9 %custom-call.149 = f32[4,128,128]{2,1,0:T(8,128)S(1)} custom-call(f32[4,128,128]{2,1,0:T(8,128)S(1)} %get-tuple-element.207), custom_call_target="Cholesky" | custom-call | tf_op jit(solution)/shard_map/jvp(vmap(jit(cholesky)))/cholesky/custom-call.1 | solution.py:18
  464.0 48.1 %custom-call.140 = f32[4,128,128]{2,1,0:T(8,128)S(1)} custom-call(f32[4,128,128]{2,1,0:T(8,128)} %get-tuple-element.208), custom_call_target="Cholesky" | custom-call | tf_op jit(solution)/shard_map/jvp(vmap(jit(cholesky)))/cholesky/custom-call.1 | solution.py:18
  570.1 40.9 %custom-call.100 = f32[4,1,128,128]{2,3,1,0:T(8,128)} custom-call(f32[4,1,128,128]{3,2,1,0:T(8,128)} %select_bitcast_fusion.13), custom_call_target="InvertDiagBlocksLowerTriangular" | custom-call | tf_op jit(solution)/shard_map/vmap(jit(_cho_solve))/triangular_solve/custom-call.2 | solution.py:19
  611.0 40.8 %custom-call.109 = f32[4,1,128,128]{2,3,1,0:T(8,128)} custom-call(f32[4,1,128,128]{3,2,1,0:T(8,128)} %get-tuple-element.199), custom_call_target="InvertDiagBlocksLowerTriangular" | custom-call | tf_op jit(solution)/shard_map/vmap(jit(_cho_solve))/triangular_solve/custom-call.2 | solution.py:19
  668.5 40.1 %custom-call.152 = f32[4,1,128,128]{2,3,1,0:T(8,128)S(1)} custom-call(f32[4,1,128,128]{3,2,1,0:T(8,128)} %get-tuple-element.195), custom_call_target="InvertDiagBlocksLowerTriangular" | custom-call | tf_op jit(solution)/shard_map/transpose(jvp(vmap(jit(_cho_solve))))/triangular_solve/custom-call.0 | solution.py:19
  720.8 40.2 %custom-call.106 = f32[4,1,128,128]{2,3,1,0:T(8,128)S(1)} custom-call(f32[4,1,128,128]{3,2,1,0:T(8,128)} %get-tuple-element.198), custom_call_target="InvertDiagBlocksLowerTriangular" | custom-call | tf_op jit(solution)/shard_map/vmap(jit(_cho_solve))/triangular_solve/custom-call.2 | solution.py:19
  775.0 40.1 %custom-call.116 = f32[4,1,128,128]{2,3,1,0:T(8,128)S(1)} custom-call(f32[4,1,128,128]{3,2,1,0:T(8,128)} %get-tuple-element.201), custom_call_target="InvertDiagBlocksLowerTriangular" | custom-call | tf_op jit(solution)/shard_map/transpose(jvp(vmap(jit(_cho_solve))))/triangular_solve/custom-call.0 | solution.py:19
  815.1 40.7 %custom-call.143 = f32[4,1,128,128]{2,3,1,0:T(8,128)} custom-call(f32[4,1,128,128]{3,2,1,0:T(8,128)} %get-tuple-element.203), custom_call_target="InvertDiagBlocksLowerTriangular" | custom-call | tf_op jit(solution)/shard_map/transpose(jvp(vmap(jit(_cho_solve))))/triangular_solve/custom-call.0 | solution.py:19
  952.7 40.1 %custom-call.103 = f32[4,1,128,128]{2,3,1,0:T(8,128)S(1)} custom-call(f32[4,1,128,128]{3,2,1,0:T(8,128)} %get-tuple-element.197), custom_call_target="InvertDiagBlocksLowerTriangular" | custom-call | tf_op jit(solution)/shard_map/vmap(jit(_cho_solve))/triangular_solve/custom-call.2 | solution.py:19
  1032.8 40.8 %custom-call.129 = f32[4,1,128,128]{2,3,1,0:T(8,128)} custom-call(f32[4,1,128,128]{3,2,1,0:T(8,128)} %get-tuple-element.172), custom_call_target="InvertDiagBlocksLowerTriangular" | custom-call | tf_op jit(solution)/shard_map/transpose(jvp(vmap(jit(cholesky))))/triangular_solve/custom-call.2 | solution.py:18
  1073.6 40.7 %custom-call.156 = f32[4,1,128,128]{2,3,1,0:T(8,128)} custom-call(f32[4,1,128,128]{3,2,1,0:T(8,128)} %get-tuple-element.196), custom_call_target="InvertDiagBlocksLowerTriangular" | custom-call | tf_op jit(solution)/shard_map/transpose(jvp(vmap(jit(cholesky))))/triangular_solve/custom-call.2 | solution.py:18
  1114.3 40.7 %custom-call.120 = f32[4,1,128,128]{2,3,1,0:T(8,128)} custom-call(f32[4,1,128,128]{3,2,1,0:T(8,128)} %get-tuple-element.202), custom_call_target="InvertDiagBlocksLowerTriangular" | custom-call | tf_op jit(solution)/shard_map/transpose(jvp(vmap(jit(cholesky))))/triangular_solve/custom-call.2 | solution.py:18
  1155.1 40.7 %custom-call.147 = f32[4,1,128,128]{2,3,1,0:T(8,128)} custom-call(f32[4,1,128,128]{3,2,1,0:T(8,128)} %get-tuple-element.204), custom_call_target="InvertDiagBlocksLowerTriangular" | custom-call | tf_op jit(solution)/shard_map/transpose(jvp(vmap(jit(cholesky))))/triangular_solve/custom-call.2 | solution.py:18
  1195.8 41.1 %custom-call.138 = f32[4,1,128,128]{2,3,1,0:T(8,128)} custom-call(f32[4,1,128,128]{3,2,1,0:T(8,128)} %get-tuple-element.206), custom_call_target="InvertDiagBlocksLowerTriangular" | custom-call | tf_op jit(solution)/shard_map/transpose(jvp(vmap(jit(cholesky))))/triangular_solve/custom-call.2 | solution.py:18
  1510.2 80.7 %all-reduce.3.cloned.1.call-done = (f32[4,128,128]{2,1,0:T(8,128)}, f32[1,4,128,128]{3,2,1,0:T(8,128)}, f32[1,4,128,128]{3,2,1,0:T(8,128)}, f32[1,4,128,128]{3,2,1,0:T(8,128)}, f32[1,4,128,128]{3,2,1,0:T(8,128)}) async-done(((f32[4,128,128]{2,1,0:T(8,128)}, f32[1,4,128,128]{3,2,1,0:T(8,128)}, f32[1,4,128,128]{3,2,1,0:T(8,128)}, f32[1,4,128,128]{3,2,1,0:T(8,128)}, f32[1,4,128,128]{3,2,1,0:T(8,128)}), ...) | async-done | bytes 1310736 | tf_op jit(solution)/shard_map/psum | solution.py:59
  1593.2 181.2 %reduce-scatter.2.cloned.1.call-done = f32[512,512]{1,0:T(8,128)} async-done(((f32[512,8192]{1,0:T(8,128)}), f32[512,512]{1,0:T(8,128)}) %reduce-scatter.2.cloned.1.call-update) | async-done | bytes 1048592 | tf_op jit(solution)/shard_map/reduce_scatter | solution.py:89
  (384 shorter events, 543.3 us)
Async XLA Ops:
  7.2 551.7 %copy-start = (bf16[512,512]{1,0:T(8,128)(2,1)S(1)}, bf16[512,512]{1,0:T(8,128)(2,1)}, u32[]{:S(2)}) copy-start(bf16[512,512]{1,0:T(8,128)(2,1)} %param.24) | copy-start | bytes 1572868
  7.2 1241.5 %all-gather.2.cloned.1.call-start = ((), (), s32[]{:S(2)}) async-start(), calls=%async_computation.2 | async-start | bytes 8912896 | tf_op jit(solution)/shard_map/all_gather | solution.py:91
  7.9 1583.0 %all-reduce.3.cloned.1.call-start = ((), (), s32[]{:S(2)}) async-start(), calls=%async_computation.3 | async-start | bytes 2621440 | tf_op jit(solution)/shard_map/psum | solution.py:59
  314.1 245.4 %copy-start.40 = (f32[4,128,128]{2,1,0:T(8,128)}, f32[4,128,128]{2,1,0:T(8,128)S(1)}, u32[]{:S(2)}) copy-start(f32[4,128,128]{2,1,0:T(8,128)S(1)} %custom-call.113) | copy-start | bytes 786436
  367.2 192.3 %copy-start.43 = (f32[4,128,128]{2,1,0:T(8,128)}, f32[4,128,128]{2,1,0:T(8,128)S(1)}, u32[]{:S(2)}) copy-start(f32[4,128,128]{2,1,0:T(8,128)S(1)} %custom-call.131) | copy-start | bytes 786436
  414.1 143.3 %copy-start.41 = (f32[4,128,128]{2,1,0:T(8,128)}, f32[4,128,128]{2,1,0:T(8,128)S(1)}, u32[]{:S(2)}) copy-start(f32[4,128,128]{2,1,0:T(8,128)S(1)} %custom-call.122) | copy-start | bytes 786436
  566.6 88.8 %collective-permute-start = (f32[512,4,64]{0,2,1:T(8,128)}, f32[512,4,64]{0,2,1:T(8,128)}, u32[]{:S(2)}, u32[]{:S(2)}) collective-permute-start(f32[512,4,64]{0,2,1:T(8,128)} %copy.630), channel_id=1, source_target_pairs={{0,1},{1,0},{2,3},{3,2},{4,5},{5,4},{6,7},{7,6},{8,9},{9,8},{10,11... | collective-permute-start | bytes 1572872 | tf_op jit(solution)/shard_map/ppermute | solution.py:8
  666.2 45.9 %collective-permute-start.1 = (f32[512,4,64]{0,2,1:T(8,128)}, f32[512,4,64]{0,2,1:T(8,128)}, u32[]{:S(2)}, u32[]{:S(2)}) collective-permute-start(f32[512,4,64]{0,2,1:T(8,128)} %copy.634), channel_id=1, source_target_pairs={{0,1},{1,0},{2,3},{3,2},{4,5},{5,4},{6,7},{7,6},{8,9},{9,8},{10,11... | collective-permute-start | bytes 1572872 | tf_op jit(solution)/shard_map/ppermute | solution.py:8
  719.3 43.4 %collective-permute-start.2 = (f32[512,4,64]{0,2,1:T(8,128)S(1)}, f32[512,4,64]{0,2,1:T(8,128)}, u32[]{:S(2)}, u32[]{:S(2)}) collective-permute-start(f32[512,4,64]{0,2,1:T(8,128)S(1)} %copy.637), channel_id=1, source_target_pairs={{0,2},{1,3},{2,0},{3,1},{4,6},{5,7},{6,4},{7,5},{8,10},{9,11},{10,... | collective-permute-start | bytes 1572872 | tf_op jit(solution)/shard_map/ppermute | solution.py:8
  772.3 128.3 %collective-permute-start.3 = (f32[512,4,64]{0,2,1:T(8,128)}, f32[512,4,64]{0,2,1:T(8,128)}, u32[]{:S(2)}, u32[]{:S(2)}) collective-permute-start(f32[512,4,64]{0,2,1:T(8,128)} %copy.641), channel_id=1, source_target_pairs={{0,2},{1,3},{2,0},{3,1},{4,6},{5,7},{6,4},{7,5},{8,10},{9,11},{10,... | collective-permute-start | bytes 1572872 | tf_op jit(solution)/shard_map/ppermute | solution.py:8
  896.0 103.6 %copy-start.1 = (f32[4,1,128,128]{2,3,1,0:T(8,128)}, f32[4,1,128,128]{2,3,1,0:T(8,128)S(1)}, u32[]{:S(2)}) copy-start(f32[4,1,128,128]{2,3,1,0:T(8,128)S(1)} %custom-call.134) | copy-start | bytes 786436
  908.5 87.0 %collective-permute-start.4 = (f32[512,4,64]{0,2,1:T(8,128)}, f32[512,4,64]{0,2,1:T(8,128)}, u32[]{:S(2)}, u32[]{:S(2)}) collective-permute-start(f32[512,4,64]{0,2,1:T(8,128)} %copy.644), channel_id=1, source_target_pairs={{0,4},{1,5},{2,6},{3,7},{4,0},{5,1},{6,2},{7,3},{8,12},{9,13},{10,... | collective-permute-start | bytes 1572872 | tf_op jit(solution)/shard_map/ppermute | solution.py:8
  1006.4 13.8 collective-permute-start.5
  1027.4 213.8 %collective-permute-start.6 = (f32[512,4,64]{0,2,1:T(8,128)S(1)}, f32[512,4,64]{0,2,1:T(8,128)}, u32[]{:S(2)}, u32[]{:S(2)}) collective-permute-start(f32[512,4,64]{0,2,1:T(8,128)S(1)} %copy.651), channel_id=1, source_target_pairs={{0,8},{1,9},{2,10},{3,11},{4,12},{5,13},{6,14},{7,15},{8,0},{9,1},... | collective-permute-start | bytes 1572872 | tf_op jit(solution)/shard_map/ppermute | solution.py:8
  1248.2 22.8 %collective-permute-start.7 = (bf16[512,4,64]{0,2,1:T(8,128)(2,1)}, bf16[512,4,64]{0,2,1:T(8,128)(2,1)}, u32[]{:S(2)}, u32[]{:S(2)}) collective-permute-start(bf16[512,4,64]{0,2,1:T(8,128)(2,1)} %copy.655), channel_id=1, source_target_pairs={{0,8},{1,9},{2,10},{3,11},{4,12},{5,13},{6,14},{7,15},{8,0},{9,1},... | collective-permute-start | bytes 786440 | tf_op jit(solution)/shard_map/ppermute | solution.py:8
  1267.3 13.9 collective-permute-start.8
  1293.0 14.9 collective-permute-start.9
  1315.1 11.0 collective-permute-start.10
  1339.4 12.1 collective-permute-start.11
  1359.5 10.2 collective-permute-start.12
  1388.3 9.5 collective-permute-start.13
  1405.9 8.0 collective-permute-start.14
  1431.1 9.6 collective-permute-start.15
  1498.5 276.0 %reduce-scatter.2.cloned.1.call-start = ((), (), s32[]{:S(2)}) async-start(), calls=%async_computation.1 | async-start | bytes 17825792 | tf_op jit(solution)/shard_map/reduce_scatter | solution.py:89
  (42 other events, 546.5 us)
Sparse Core Ops, SparseCore 0:
  9.7 54.3 all-gather.1
  1498.6 92.3 all-reduce.2
  1593.9 180.4 reduce-scatter.1
where the time goes:
time: 1800 us; the launch traced here: 1780 us
  other arithmetic  1160 us (64%)
  waiting for transfers between devices  287 us (16%)
  matrix products  186 us (10%)
  local copies, waits for them, and re-layouts  117 us (6%)
  starting transfers between devices  19.1 us (1%)
    another operation x28, other arithmetic, cayley_block(): chol_factor = jnp.linalg.cholesky(spd_matrix)  685 us
    another operation x11, other arithmetic, cayley_block(): return jax.scipy.linalg.cho_solve((chol_factor, True), numerator.T).T  404 us
    reduce_scatter x1, waiting for transfers between devices, body(): lax.psum_scatter(partial_out, 'tensor', scatter_dimension=1, tiled=True)  181 us
    psum x1, waiting for transfers between devices, sum_data(): return lax.psum(value, 'dp')  80.7 us
    another operation x40, matrix products, cayley_block(): return jax.scipy.linalg.cho_solve((chol_factor, True), numerator.T).T  58.6 us
  transfers between devices with their start and end apart: 19, of which 7 were waited for; matrix products, arithmetic and copies ran while one was open for 74% of the time, Pallas kernels for 0%

commit v1 on v0

--- a/solution.py
+++ b/solution.py
@@ -1,6 +1,8 @@
 import jax
 import jax.numpy as jnp
 from jax import lax
+from jax.experimental import pallas as pl
+from jax.experimental.pallas import tpu as pltpu
 from jax.sharding import PartitionSpec as P
 
 
@@ -8,24 +10,45 @@
     return lax.ppermute(shard, axis, [(i, i ^ 1 << stride) for i in range(lax.axis_size(axis))])
 
 
-def cayley_block(param):
-    highest = lax.Precision.HIGHEST
-    skew = param - param.T
-    identity = jnp.eye(param.shape[0], dtype=param.dtype)
-    one_minus = identity - skew
-    spd_matrix = identity - jnp.dot(skew, skew, precision=highest)
-    numerator = jnp.dot(one_minus, one_minus, precision=highest)
-    chol_factor = jnp.linalg.cholesky(spd_matrix)
-    return jax.scipy.linalg.cho_solve((chol_factor, True), numerator.T).T
+def inverse_kernel(param_ref, out_ref):
+    count, size, _ = param_ref.shape
+    rows = lax.broadcasted_iota(jnp.int32, (size, size), 0)
+    lanes = lax.broadcasted_iota(jnp.int32, (size, size), 1)
+    row_lanes = lax.broadcasted_iota(jnp.int32, (1, size), 1)
+    identity = jnp.where(rows == lanes, 1.0, 0.0)
+    for at in range(count):
+        param = param_ref[at]
+        out_ref[at] = identity + param - param.T
+
+    def eliminate(k, carry):
+        for at in range(count):
+            matrix = out_ref[at]
+            row = out_ref[at, pl.ds(k, 1), :]
+            hit = lanes == k
+            column = jnp.sum(jnp.where(hit, matrix, 0.0), axis=1, keepdims=True)
+            pivot = jnp.sum(jnp.where(row_lanes == k, row, 0.0), axis=1, keepdims=True)
+            scale = 1.0 / pivot
+            new_row = jnp.where(row_lanes == k, scale, row * scale)
+            out_ref[at] = jnp.where(hit, 0.0, matrix) - column * new_row
+            out_ref[at, pl.ds(k, 1), :] = new_row
+        return carry
+
+    lax.fori_loop(0, size, eliminate, 0)
 
 
-def cayley_many(params):
-    return jax.vmap(cayley_block)(params)
+def inverse_many(params):
+    return pl.pallas_call(
+        inverse_kernel,
+        out_shape=jax.ShapeDtypeStruct(params.shape, jnp.float32),
+        compiler_params=pltpu.CompilerParams(vmem_limit_bytes=32 << 20),
+    )(params)
 
 
-def cayley_pull(param, matrix_grad):
-    unused, pullback = jax.vjp(cayley_many, param)
-    return pullback(matrix_grad)[0]
+def pull_many(inverse, matrix_grad):
+    highest = lax.Precision.HIGHEST
+    left = jnp.einsum("nji,njk->nik", inverse, matrix_grad, precision=highest)
+    full = jnp.einsum("nik,njk->nij", left, inverse, precision=highest)
+    return -2.0 * (full - full.transpose(0, 2, 1))
 
 
 def split_halves(state, upper_side, blocks_dev, half_block):
@@ -67,8 +90,11 @@
     blocks_dev = local_param.shape[0]
     levels = lax.axis_size("tensor").bit_length() - 1
     position = lax.axis_index("tensor")
-    local_rot = cayley_many(local_param)
-    cross_rot = [cayley_many(cross_param[level_idx]) for level_idx in range(levels)]
+    params = jnp.concatenate([local_param, cross_param.reshape(-1, block, block)])
+    inverse = inverse_many(params)
+    rotations = 2.0 * inverse - jnp.eye(block, dtype=jnp.float32)
+    local_rot = rotations[:blocks_dev]
+    cross_rot = rotations[blocks_dev:].reshape(levels, blocks_dev, block, block)
     inputs = tokens.astype(jnp.float32).reshape(token_count, blocks_dev, block)
     state = jnp.einsum("tci,cij->tcj", inputs, local_rot, precision=highest).reshape(
         token_count, rows_dev
@@ -106,14 +132,12 @@
         keep_part, give_part = split_pair(back_vector, upper_side, half_block)
         returned = from_partner(give_part, "tensor", level_idx)
         grad_state = merge_halves(keep_part, returned, upper_side)
-        param_grad = cayley_pull(cross_param[level_idx], matrix_grad)
-        param_grad = sum_data(param_grad)
-        cross_grads[level_idx] = param_grad
+        cross_grads[level_idx] = matrix_grad
     grad_blocks = grad_state.reshape(token_count, blocks_dev, block)
     local_matrix = jnp.einsum("tci,tcj->cij", inputs, grad_blocks, precision=highest)
-    local_grad = cayley_pull(local_param, local_matrix)
-    local_grad = sum_data(local_grad)
-    cross_grad = jnp.stack(cross_grads)
+    grads = pull_many(inverse, sum_data(jnp.concatenate([local_matrix] + cross_grads)))
+    local_grad = grads[:blocks_dev]
+    cross_grad = grads[blocks_dev:].reshape(levels, blocks_dev, block, block)
     return (output, local_grad, cross_grad)
 
 

time: 1800 us -> 791 us (0.44)
  other arithmetic: 1160 us -> 56.5 us
  Pallas kernels: 0 us -> 247 us
  matrix products: 186 us -> 57.4 us
  local copies, waits for them, and re-layouts: 117 us -> 80.2 us
    another operation x44 -> x0, other arithmetic: 1100 us -> none  [the longest x28 685 us: cayley_block(): chol_factor = jnp.linalg.cholesky(spd_matrix)]
    pallas_call x0 -> x1, Pallas kernels: none -> 247 us  [inverse_many(): pl.pallas_call(inverse_kernel, out_shape=jax.ShapeDtypeStruct(params.shap...]
    another operation x50 -> x0, matrix products: 77.9 us -> none  [the longest x40 58.6 us: cayley_block(): return jax.scipy.linalg.cho_solve((chol_factor, True), numerator.T).T]
    dot_general x45 -> x2, matrix products: 56.1 us -> 6.41 us  [the longest x1 3.57 us: pull_many(): left = jnp.einsum('nji,njk->nik', inverse, matrix_grad, precision=highest)]
    ppermute x16, waiting for transfers between devices: 24.5 us -> 50 us  [from_partner(): lax.ppermute(shard, axis, [(i, i ^ 1 << stride) for i in range(lax.axis_s...]
  transfers between devices with their start and end apart: 19 -> 19, of which waited for: 7 -> 11; matrix products, arithmetic and copies ran while one was open for 74% -> 17% of each run, Pallas kernels for 0% -> 32%
where the time goes in v1:
time: 791 us; the launch traced here: 777 us
  waiting for transfers between devices  303 us (38%)
  Pallas kernels  247 us (31%)
  local copies, waits for them, and re-layouts  80.2 us (10%)
  matrix products  57.4 us (7%)
  other arithmetic  56.5 us (7%)
  starting transfers between devices  18.5 us (2%)
  between operations  14.5 us (2%)
    pallas_call x1, Pallas kernels, inverse_many(): pl.pallas_call(inverse_kernel, out_shape=jax.ShapeDtypeStruct(params.shap...  247 us
    reduce_scatter x1, waiting for transfers between devices, body(): lax.psum_scatter(partial_out, 'tensor', scatter_dimension=1, tiled=True)  173 us
    psum x1, waiting for transfers between devices, sum_data(): return lax.psum(value, 'dp')  79.3 us
    ppermute x16, waiting for transfers between devices, from_partner(): lax.ppermute(shard, axis, [(i, i ^ 1 << stride) for i in range(lax.axis_s...  50 us
    ppermute x16, local copies, waits for them, and re-layouts, from_partner(): lax.ppermute(shard, axis, [(i, i ^ 1 << stride) for i in range(lax.axis_s...  31.5 us
    select_n x8, other arithmetic, split_halves(): other_part = jnp.where(upper_side, halves[:, 0], halves[:, 1])  25.1 us
    ppermute x16, starting transfers between devices, from_partner(): lax.ppermute(shard, axis, [(i, i ^ 1 << stride) for i in range(lax.axis_s...  18.4 us
  transfers between devices with their start and end apart: 19, of which 11 were waited for; matrix products, arithmetic and copies ran while one was open for 17% of the time, Pallas kernels for 32%

profile of v1, /device:TPU:6, one launch (start us, length us, event | category | flops | bytes accessed | tf_op | source)
XLA Modules:
  0.0 776.9 jit_solution(13048657979411000086)
XLA Ops:
  9.4 247.1 %shard_map.76 = f32[20,128,128]{2,1,0:T(8,128)S(1)} custom-call(f32[20,128,128]{2,1,0:T(8,128)S(1)} %pad_maximum_fusion.1.param_ref), custom_call_target="tpu_custom_call" | custom-call | tf_op jit(solution)/shard_map/pallas_call | solution.py:40
  279.2 3.3 broadcast_select_fusion.19
  284.9 13.4 %collective-permute-done.2 = f32[512,4,64]{0,2,1:T(8,128)S(1)} collective-permute-done((f32[512,4,64]{0,2,1:T(8,128)S(1)}, f32[512,4,64]{0,2,1:T(8,128)S(1)}, u32[]{:S(2)}, u32[]{:S(2)}) %collective-permute-start.2) | collective-permute-done | bytes 524320 | tf_op jit(solution)/shard_map/ppermute | solution.py:10
  301.4 9.4 %fusion.25 = f32[512,512]{0,1:T(8,128)S(1)} fusion(bf16[512,8192]{1,0:T(8,128)(2,1)} %all-gather.2.cloned.1.call-done, bf16[512,8192]{1,0:T(8,128)(2,1)} %param.6), kind=kOutput, calls=%fused_computation.116 | convolution fusion | flops 4294967296 | bytes 17825792 | tf_op jit(solution)/shard_map/dot_general | solution.py:116
  327.8 6.6 collective-permute-done.8
  348.9 3.3 broadcast_select_fusion.31
  354.6 6.4 collective-permute-done.9
  363.4 3.3 broadcast_select_fusion.25
  375.0 5.4 collective-permute-done.10
  394.8 7.5 collective-permute-done.11
  404.7 4.1 broadcast_select_fusion.13
  414.3 3.3 broadcast_select_fusion.37
  419.1 3.4 collective-permute-start.6
  433.9 6.0 collective-permute-done.13
  442.2 3.3 broadcast_select_fusion.5
  474.0 3.3 copy.113
  479.9 4.8 convolution_dynamic-update-slice_fusion.3
  484.8 3.1 convolution_dynamic-update-slice_fusion.2
  487.9 3.1 convolution_dynamic-update-slice_fusion.1
  491.1 3.3 convolution_dynamic-update-slice_fusion
  495.4 11.6 %fusion.24 = f32[512,8192]{1,0:T(8,128)} fusion(bf16[512,512]{0,1:T(8,128)(2,1)S(1)} %bitcast.71, bf16[512,8192]{1,0:T(8,128)(2,1)} %param.6), kind=kOutput, calls=%fused_computation.115 | convolution fusion | flops 4294967296 | bytes 25690112 | tf_op jit(solution)/shard_map/dot_general | solution.py:114
  507.1 79.3 %all-reduce.2.cloned.1.call-done = f32[20,128,128]{1,2,0:T(8,128)} async-done(((f32[20,128,128]{1,2,0:T(8,128)}), f32[20,128,128]{1,2,0:T(8,128)}) %all-reduce.2.cloned.1.call-update) | async-done | bytes 1310736 | tf_op jit(solution)/shard_map/psum | solution.py:82
  586.3 3.6 fusion.26
  597.5 172.7 %reduce-scatter.2.cloned.1.call-done = f32[512,512]{1,0:T(8,128)} async-done(((f32[512,8192]{1,0:T(8,128)}), f32[512,512]{1,0:T(8,128)}) %reduce-scatter.2.cloned.1.call-update) | async-done | bytes 1048592 | tf_op jit(solution)/shard_map/reduce_scatter | solution.py:115
  (176 shorter events, 151.9 us)
Async XLA Ops:
  7.2 249.3 %copy-start = (bf16[512,512]{1,0:T(8,128)(2,1)S(1)}, bf16[512,512]{1,0:T(8,128)(2,1)}, u32[]{:S(2)}) copy-start(bf16[512,512]{1,0:T(8,128)(2,1)} %param.5) | copy-start | bytes 1572868
  7.2 294.2 %all-gather.2.cloned.1.call-start = ((), (), s32[]{:S(2)}) async-start(), calls=%async_computation.2 | async-start | bytes 8912896 | tf_op jit(solution)/shard_map/all_gather | solution.py:117
  7.9 578.4 %all-reduce.2.cloned.1.call-start = ((), (), s32[]{:S(2)}) async-start(), calls=%async_computation.3 | async-start | bytes 2621440 | tf_op jit(solution)/shard_map/psum | solution.py:82
  264.6 2.1 collective-permute-start
  274.6 2.2 collective-permute-start.1
  284.0 14.3 %collective-permute-start.2 = (f32[512,4,64]{0,2,1:T(8,128)S(1)}, f32[512,4,64]{0,2,1:T(8,128)S(1)}, u32[]{:S(2)}, u32[]{:S(2)}) collective-permute-start(f32[512,4,64]{0,2,1:T(8,128)S(1)} %copy.58), channel_id=1, source_target_pairs={{0,2},{1,3},{2,0},{3,1},{4,6},{5,7},{6,4},{7,5},{8,10},{9,11},{10,... | collective-permute-start | bytes 1572872 | tf_op jit(solution)/shard_map/ppermute | solution.py:10
  319.2 15.2 %collective-permute-start.8 = (f32[512,4,64]{0,2,1:T(8,128)}, f32[512,4,64]{0,2,1:T(8,128)}, u32[]{:S(2)}, u32[]{:S(2)}) collective-permute-start(f32[512,4,64]{0,2,1:T(8,128)} %copy.85), channel_id=1, source_target_pairs={{0,8},{1,9},{2,10},{3,11},{4,12},{5,13},{6,14},{7,15},{8,0},{9,1},... | collective-permute-start | bytes 1572872 | tf_op jit(solution)/shard_map/ppermute | solution.py:10
  326.7 19.8 %collective-permute-start.3 = (f32[512,4,64]{0,2,1:T(8,128)S(1)}, f32[512,4,64]{0,2,1:T(8,128)}, u32[]{:S(2)}, u32[]{:S(2)}) collective-permute-start(f32[512,4,64]{0,2,1:T(8,128)S(1)} %copy.63), channel_id=1, source_target_pairs={{0,2},{1,3},{2,0},{3,1},{4,6},{5,7},{6,4},{7,5},{8,10},{9,11},{10,... | collective-permute-start | bytes 1572872 | tf_op jit(solution)/shard_map/ppermute | solution.py:10
  344.5 16.4 %collective-permute-start.9 = (f32[512,4,64]{0,2,1:T(8,128)}, f32[512,4,64]{0,2,1:T(8,128)}, u32[]{:S(2)}, u32[]{:S(2)}) collective-permute-start(f32[512,4,64]{0,2,1:T(8,128)} %copy.89), channel_id=1, source_target_pairs={{0,8},{1,9},{2,10},{3,11},{4,12},{5,13},{6,14},{7,15},{8,0},{9,1},... | collective-permute-start | bytes 1572872 | tf_op jit(solution)/shard_map/ppermute | solution.py:10
  352.2 11.2 %copy-start.2 = (f32[512,4,128]{2,0,1:T(8,128)S(1)}, f32[512,4,128]{2,0,1:T(8,128)}, u32[]{:S(2)}) copy-start(f32[512,4,128]{2,0,1:T(8,128)} %copy-done.1) | copy-start | bytes 3145732
  353.8 17.0 %collective-permute-start.4 = (f32[512,4,64]{0,2,1:T(8,128)S(1)}, f32[512,4,64]{0,2,1:T(8,128)}, u32[]{:S(2)}, u32[]{:S(2)}) collective-permute-start(f32[512,4,64]{0,2,1:T(8,128)S(1)} %copy.66), channel_id=1, source_target_pairs={{0,4},{1,5},{2,6},{3,7},{4,0},{5,1},{6,2},{7,3},{8,12},{9,13},{10,... | collective-permute-start | bytes 1572872 | tf_op jit(solution)/shard_map/ppermute | solution.py:10
  369.0 11.4 %collective-permute-start.10 = (f32[512,4,64]{0,2,1:T(8,128)}, f32[512,4,64]{0,2,1:T(8,128)}, u32[]{:S(2)}, u32[]{:S(2)}) collective-permute-start(f32[512,4,64]{0,2,1:T(8,128)} %copy.92), channel_id=1, source_target_pairs={{0,4},{1,5},{2,6},{3,7},{4,0},{5,1},{6,2},{7,3},{8,12},{9,13},{10,... | collective-permute-start | bytes 1572872 | tf_op jit(solution)/shard_map/ppermute | solution.py:10
  387.1 15.2 %collective-permute-start.11 = (f32[512,4,64]{0,2,1:T(8,128)}, f32[512,4,64]{0,2,1:T(8,128)}, u32[]{:S(2)}, u32[]{:S(2)}) collective-permute-start(f32[512,4,64]{0,2,1:T(8,128)} %copy.96), channel_id=1, source_target_pairs={{0,4},{1,5},{2,6},{3,7},{4,0},{5,1},{6,2},{7,3},{8,12},{9,13},{10,... | collective-permute-start | bytes 1572872 | tf_op jit(solution)/shard_map/ppermute | solution.py:10
  394.0 17.9 %collective-permute-start.5 = (f32[512,4,64]{0,2,1:T(8,128)S(1)}, f32[512,4,64]{0,2,1:T(8,128)}, u32[]{:S(2)}, u32[]{:S(2)}) collective-permute-start(f32[512,4,64]{0,2,1:T(8,128)S(1)} %copy.71), channel_id=1, source_target_pairs={{0,4},{1,5},{2,6},{3,7},{4,0},{5,1},{6,2},{7,3},{8,12},{9,13},{10,... | collective-permute-start | bytes 1572872 | tf_op jit(solution)/shard_map/ppermute | solution.py:10
  411.1 11.4 %collective-permute-start.12 = (f32[512,4,64]{0,2,1:T(8,128)}, f32[512,4,64]{0,2,1:T(8,128)}, u32[]{:S(2)}, u32[]{:S(2)}) collective-permute-start(f32[512,4,64]{0,2,1:T(8,128)} %copy.99), channel_id=1, source_target_pairs={{0,2},{1,3},{2,0},{3,1},{4,6},{5,7},{6,4},{7,5},{8,10},{9,11},{10,... | collective-permute-start | bytes 1572872 | tf_op jit(solution)/shard_map/ppermute | solution.py:10
  419.1 12.4 %collective-permute-start.6 = (f32[512,4,64]{0,2,1:T(8,128)S(1)}, f32[512,4,64]{0,2,1:T(8,128)}, u32[]{:S(2)}, u32[]{:S(2)}) collective-permute-start(f32[512,4,64]{0,2,1:T(8,128)S(1)} %copy.74), channel_id=1, source_target_pairs={{0,8},{1,9},{2,10},{3,11},{4,12},{5,13},{6,14},{7,15},{8,0},{9,1},... | collective-permute-start | bytes 1572872 | tf_op jit(solution)/shard_map/ppermute | solution.py:10
  430.4 9.5 %collective-permute-start.13 = (f32[512,4,64]{0,2,1:T(8,128)}, f32[512,4,64]{0,2,1:T(8,128)}, u32[]{:S(2)}, u32[]{:S(2)}) collective-permute-start(f32[512,4,64]{0,2,1:T(8,128)} %copy.103), channel_id=1, source_target_pairs={{0,2},{1,3},{2,0},{3,1},{4,6},{5,7},{6,4},{7,5},{8,10},{9,11},{10,... | collective-permute-start | bytes 1572872 | tf_op jit(solution)/shard_map/ppermute | solution.py:10
  447.2 5.1 collective-permute-start.14
  451.1 10.5 %collective-permute-start.7 = (bf16[512,4,64]{0,2,1:T(8,128)(2,1)}, bf16[512,4,64]{0,2,1:T(8,128)(2,1)}, u32[]{:S(2)}, u32[]{:S(2)}) collective-permute-start(bf16[512,4,64]{0,2,1:T(8,128)(2,1)} %copy.79), channel_id=1, source_target_pairs={{0,8},{1,9},{2,10},{3,11},{4,12},{5,13},{6,14},{7,15},{8,0},{9,1},... | collective-permute-start | bytes 786440 | tf_op jit(solution)/shard_map/ppermute | solution.py:10
  460.1 8.4 %collective-permute-start.15 = (f32[512,4,64]{0,2,1:T(8,128)}, f32[512,4,64]{0,2,1:T(8,128)}, u32[]{:S(2)}, u32[]{:S(2)}) collective-permute-start(f32[512,4,64]{0,2,1:T(8,128)} %copy.110), channel_id=1, source_target_pairs={{0,1},{1,0},{2,3},{3,2},{4,5},{5,4},{6,7},{7,6},{8,9},{9,8},{10,11... | collective-permute-start | bytes 1572872 | tf_op jit(solution)/shard_map/ppermute | solution.py:10
  474.0 5.9 copy-start.11
  479.9 4.8 copy-start.12
  479.9 4.8 copy-start.13
  494.4 275.8 %reduce-scatter.2.cloned.1.call-start = ((), (), s32[]{:S(2)}) async-start(), calls=%async_computation.1 | async-start | bytes 17825792 | tf_op jit(solution)/shard_map/reduce_scatter | solution.py:115
  (28 other events, 61.1 us)
Sparse Core Ops, SparseCore 0:
  9.7 54.4 all-gather.1
  494.5 91.7 all-reduce.1
  589.3 180.8 reduce-scatter.1

commit v2 on v1

v2 whole, which is shorter than its diff:
```python
import functools

import jax
import jax.numpy as jnp
from jax import lax
from jax.experimental import pallas as pl
from jax.experimental.pallas import tpu as pltpu
from jax.sharding import PartitionSpec as P

MESH = pl.DeviceIdType.MESH
F32 = jnp.float32
BF16 = jnp.bfloat16
ANY = pl.BlockSpec(memory_space=pl.ANY)
VMEM = pl.BlockSpec(memory_space=pltpu.VMEM)
DMA = pltpu.SemaphoreType.DMA
GROUP = 16
CHIPS = 8
HALF = 64
BLOCK = 128
ROWS = 256


def params_of(identity, vmem=60):
    return pltpu.CompilerParams(
        collective_id=identity, has_side_effects=True, vmem_limit_bytes=vmem << 20
    )


def meet(peers):
    barrier = pltpu.get_barrier_semaphore()
    for peer in peers:
        pl.semaphore_signal(barrier, inc=1, device_id={"tensor": peer}, device_id_type=MESH)
    pl.semaphore_wait(barrier, len(peers))


def push(src, dst, send, recv, peer):
    return pltpu.make_async_remote_copy(
        src_ref=src, dst_ref=dst, send_sem=send, recv_sem=recv,
        device_id={"tensor": peer}, device_id_type=MESH,
    )


def arrived(ref, sem):
    pltpu.make_async_copy(ref, ref, sem).wait()


def split(value):
    high = value.astype(BF16)
    return high, (value - high.astype(F32)).astype(BF16)


def dot(a, b, dims=(((1,), (0,)), ((), ()))):
    return lax.dot_general(a, b, dims, preferred_element_type=F32)


NT = (((1,), (1,)), ((), ()))
TN = (((0,), (0,)), ((), ()))


def dot3(a, b, dims=(((1,), (0,)), ((), ()))):
    return dot(a[0], b[0], dims) + (dot(a[0], b[1], dims) + dot(a[1], b[0], dims))


def spread_kernel(tok_ref, froz_ref, x_ref, cat_ref, tsend, trecv, fsend, frecv, local, flocal):
    me = lax.axis_index("tensor")
    core = lax.rem(me, 2)
    partner = me + 1 - 2 * core
    others = [lax.rem(me + k, GROUP) for k in range(1, GROUP)]
    meet(others)

    def token_slice(peer):
        column = pl.multiple_of((peer // 4) * BLOCK, BLOCK)
        row = pl.multiple_of(lax.rem(peer, 2) * ROWS, ROWS)
        return tok_ref.at[pl.ds(row, ROWS), pl.ds(column, BLOCK)]

    sends = []
    for k, peer in enumerate(others):
        copy = push(token_slice(peer), x_ref.at[me], tsend.at[k], trecv.at[me], peer)
        copy.start()
        sends.append(copy)
    for j in range(CHIPS):
        theirs = pl.multiple_of((2 * j + 1 - core) * 512, 512)
        copy = push(
            froz_ref.at[:, :, pl.ds(theirs, 512)], cat_ref.at[:, core, :, pl.ds(j * 512, 512)],
            fsend.at[j], frecv.at[j], partner,
        )
        copy.start()
        sends.append(copy)
    own = pltpu.make_async_copy(token_slice(me), x_ref.at[me], local)
    own.start()
    keeps = []
    for j in range(CHIPS):
        mine = pl.multiple_of((2 * j + core) * 512, 512)
        copy = pltpu.make_async_copy(
            froz_ref.at[:, :, pl.ds(mine, 512)], cat_ref.at[:, core, :, pl.ds(j * 512, 512)],
            flocal.at[j],
        )
        copy.start()
        keeps.append(copy)
    own.wait()
    for copy in keeps:
        copy.wait()
    for copy in sends:
        copy.wait_send()
    for peer in others:
        arrived(x_ref.at[peer], trecv.at[peer])
    for j in range(CHIPS):
        arrived(cat_ref.at[:, 1 - core, :, pl.ds(j * 512, 512)], frecv.at[j])


def spread(tokens, frozen):
    return pl.pallas_call(
        spread_kernel,
        out_shape=(
            jax.ShapeDtypeStruct((GROUP, ROWS, BLOCK), BF16),
            jax.ShapeDtypeStruct((CHIPS, 2, HALF, 4096), BF16),
        ),
        in_specs=[ANY, ANY],
        out_specs=(ANY, ANY),
        scratch_shapes=[
            DMA((GROUP,)), DMA((GROUP,)), DMA((CHIPS,)), DMA((CHIPS,)), DMA, DMA((CHIPS,)),
        ],
        compiler_params=params_of(0),
    )(tokens, frozen.reshape(CHIPS, HALF, 8192))


def inverse_kernel(param_ref, out_ref, rot_ref):
    count, size, _ = param_ref.shape
    step = 32
    rows = lax.broadcasted_iota(jnp.int32, (size, size), 0)
    lanes = lax.broadcasted_iota(jnp.int32, (size, size), 1)
    panel_rows = lax.broadcasted_iota(jnp.int32, (step, size), 0)
    panel_lanes = lax.broadcasted_iota(jnp.int32, (step, size), 1)
    identity = jnp.where(rows == lanes, 1.0, 0.0)
    for at in range(count):
        param = param_ref[at]
        out_ref[at] = identity + param - param.T

    def eliminate(block_at, carry):
        start = pl.multiple_of(block_at * step, step)
        shift = lax.rem(size - start, size)
        inside = (lanes >= start) & (lanes < start + step)
        panels = [pltpu.roll(out_ref[at, pl.ds(start, step), :], shift, 1) for at in range(count)]
        for k in range(step):
            for at in range(count):
                panel = panels[at]
                column = panel[:, k:k + 1]
                scale = 1.0 / panel[k:k + 1, k:k + 1]
                row = jnp.where(panel_lanes[:1] == k, 1.0, panel[k:k + 1, :]) * scale
                rest = jnp.where(panel_lanes == k, 0.0, panel) - column * row
                panels[at] = jnp.where(panel_rows == k, row, rest)
        panels = [pltpu.roll(panel, start, 1) for panel in panels]
        for at in range(count):
            matrix = out_ref[at]
            turned = pltpu.roll(matrix, shift, 1)[:, :step]
            out_ref[at] = jnp.where(inside, 0.0, matrix) - jnp.dot(
                turned, panels[at], precision=lax.Precision.HIGHEST, preferred_element_type=F32
            )
        for at in range(count):
            out_ref[at, pl.ds(start, step), :] = panels[at]
        return carry

    lax.fori_loop(0, size // step, eliminate, 0)
    for at in range(count):
        rotation = 2.0 * out_ref[at] - identity
        rot_ref[at] = rotation.T if at < 4 else rotation


def inverse_many(params):
    shape = jax.ShapeDtypeStruct(params.shape, F32)
    return pl.pallas_call(
        inverse_kernel,
        out_shape=(shape, shape),
        compiler_params=pltpu.CompilerParams(vmem_limit_bytes=32 << 20),
    )(params)


def pair_place(me, level):
    low = 2 ** level
    bit = lax.rem(me // low, 2)
    pair = (me // (2 * low)) * low + lax.rem(me, low)
    return bit, pair


def pair_owner(pair, level, bit):
    low = 2 ** level
    return (pair // low) * (2 * low) + bit * low + lax.rem(pair, low)


def route_kernel(rot_ref, cross_ref, local_ref, send, recv, lsend, lrecv, fsend, frecv):
    me = lax.axis_index("tensor")
    core = lax.rem(me, 2)
    chip = me // 2
    partner = me + 1 - 2 * core
    meet([lax.rem(me + k, GROUP) for k in range(1, GROUP)])

    def start(src, dst, send_sem, recv_sem, peer):
        @pl.when(peer == me)
        def _():
            pltpu.make_async_copy(src, dst, recv_sem).start()

        @pl.when(peer != me)
        def _():
            push(src, dst, send_sem, recv_sem, peer).start()

    def drain(src, dst, send_sem, recv_sem, peer):
        @pl.when(peer != me)
        def _():
            push(src, dst, send_sem, recv_sem, peer).wait_send()

    jobs = []
    for level in range(4):
        bit, pair = pair_place(me, level)
        for c in range(4):
            peer = 2 * (c + 4 * bit) + lax.rem(pair, 2)
            jobs.append((
                rot_ref.at[4 + 4 * level + c], cross_ref.at[level, pair // 2, lax.rem(pair, 2)],
                send.at[level, c], recv.at[level, pair // 2], peer,
            ))
    for c in range(4):
        for side in range(2):
            peer = 2 * (2 * c + side) + core
            jobs.append((
                rot_ref.at[c, pl.ds(side * HALF, HALF), :], local_ref.at[chip, core],
                lsend.at[c, side], lrecv.at[chip], peer,
            ))
    for job in jobs:
        start(*job)
    forwards = []
    for level in range(4):
        for q in range(4):
            arrived(cross_ref.at[level, q, core], recv.at[level, q])
        part = cross_ref.at[level, :, core]
        copy = push(part, part, fsend.at[level], frecv.at[level], partner)
        copy.start()
        forwards.append(copy)
    for q in range(CHIPS):
        arrived(local_ref.at[q, core], lrecv.at[q])
    part = local_ref.at[:, core]
    copy = push(part, part, fsend.at[4], frecv.at[4], partner)
    copy.start()
    forwards.append(copy)
    for job in jobs:
        drain(*job)
    for copy in forwards:
        copy.wait_send()
    for level in range(4):
        arrived(cross_ref.at[level, :, 1 - core], frecv.at[level])
    arrived(local_ref.at[:, 1 - core], frecv.at[4])


def route(rotations):
    return pl.pallas_call(
        route_kernel,
        out_shape=(
            jax.ShapeDtypeStruct((4, 4, 2, BLOCK, BLOCK), F32),
            jax.ShapeDtypeStruct((CHIPS, 2, HALF, BLOCK), F32),
        ),
        in_specs=[ANY],
        out_specs=(ANY, ANY),
        scratch_shapes=[
            DMA((4, 4)), DMA((4, 4)), DMA((4, 2)), DMA((CHIPS,)), DMA((5,)), DMA((5,)),
        ],
        compiler_params=params_of(1),
    )(rotations)


def mix(a, b, r):
    at = (r // 2) * BLOCK
    first, second = a[:, at:at + BLOCK], b[:, at:at + BLOCK]
    lanes = lax.broadcasted_iota(jnp.int32, first.shape, 1)
    if r % 2 == 0:
        return jnp.where(lanes < HALF, first, pltpu.roll(second, HALF, 1))
    return jnp.where(lanes < HALF, pltpu.roll(first, HALF, 1), second)


def regroup(quads):
    return [
        jnp.concatenate([mix(quads[0], quads[1], r), mix(quads[2], quads[3], r)], axis=1)
        for r in range(4)
    ]


def place_near(a, b):
    zero = jnp.zeros((BLOCK, BLOCK), F32)
    return jnp.concatenate(
        [jnp.concatenate([a, zero], axis=1), jnp.concatenate([zero, b], axis=1)], axis=0
    )


def place_far(a, b):
    lanes = lax.broadcasted_iota(jnp.int32, (BLOCK, BLOCK), 1)
    turned_a, turned_b = pltpu.roll(a, HALF, 1), pltpu.roll(b, HALF, 1)
    low = lanes < HALF
    a_rows = jnp.concatenate([jnp.where(low, a, 0.0), jnp.where(low, turned_a, 0.0)], axis=1)
    b_rows = jnp.concatenate([jnp.where(low, 0.0, turned_b), jnp.where(low, 0.0, b)], axis=1)
    return jnp.concatenate(
        [a_rows[:HALF], b_rows[:HALF], a_rows[HALF:], b_rows[HALF:]], axis=0
    )


def take_far(full):
    lanes = lax.broadcasted_iota(jnp.int32, (BLOCK, BLOCK), 1)
    low = lanes < HALF
    a_rows = jnp.concatenate([full[:HALF], full[BLOCK:BLOCK + HALF]], axis=0)
    b_rows = jnp.concatenate([full[HALF:BLOCK], full[BLOCK + HALF:]], axis=0)
    a = jnp.where(low, a_rows[:, :BLOCK], pltpu.roll(a_rows[:, BLOCK:], HALF, 1))
    b = jnp.where(low, pltpu.roll(b_rows[:, :BLOCK], HALF, 1), b_rows[:, BLOCK:])
    return a, b


def pairs_of(level, index):
    if level < 2:
        return 2 * index, 2 * index + 1
    return index, 4 + index


def forward_kernel(
    x_ref, cross_ref, local_ref, mats_ref, saved_ref, act_ref, rot_scr, send, recv, local, fsend, frecv
):
    me = lax.axis_index("tensor")
    core = lax.rem(me, 2)
    chip = me // 2
    partner = me + 1 - 2 * core
    peers = [lax.rem(me + 2 * k, GROUP) for k in range(1, CHIPS)]
    meet(peers + [partner])
    for level in range(4):
        for index in range(4):
            one, two = pairs_of(level, index)
            a = cross_ref[level, one // 2, one % 2]
            b = cross_ref[level, two // 2, two % 2]
            full = place_near(a, b) if level % 2 == 0 else place_far(a, b)
            high, low = split(full)
            mats_ref[level, index, 0] = high
            mats_ref[level, index, 1] = low
    lanes = lax.broadcasted_iota(jnp.int32, (ROWS, BLOCK), 1)
    for m in range(CHIPS):
        parts = []
        for side in range(2):
            high, low = split(jnp.concatenate([local_ref[m, side]] * 2, axis=0))
            x = x_ref[2 * m + side]
            parts.append(dot(x, high, NT) + dot(x, low, NT))
        saved_ref[0, m // 2, :, (m % 2) * BLOCK:(m % 2 + 1) * BLOCK] = jnp.where(
            lanes < HALF, parts[0], parts[1]
        )
    for level in range(4):
        outs = []
        for index in range(4):
            state = split(saved_ref[level, index])
            outs.append(dot3(state, (mats_ref[level, index, 0], mats_ref[level, index, 1])))
        if level % 2 == 1:
            outs = regroup(outs)
        for index in range(4):
            if level < 3:
                saved_ref[level + 1, index] = outs[index]
            else:
                rot_scr[:, index * 256:(index + 1) * 256] = outs[index].astype(BF16)
    row = pl.multiple_of(core * ROWS, ROWS)
    column = pl.multiple_of(chip * BLOCK, BLOCK)
    landing = act_ref.at[pl.ds(row, ROWS), pl.ds(column, BLOCK)]
    copies = []
    for k, peer in enumerate(peers):
        source = pl.multiple_of((peer // 2) * BLOCK, BLOCK)
        copy = push(rot_scr.at[:, pl.ds(source, BLOCK)], landing, send.at[k], recv.at[chip], peer)
        copy.start()
        copies.append(copy)
    own = pltpu.make_async_copy(rot_scr.at[:, pl.ds(column, BLOCK)], landing, local)
    own.start()
    own.wait()
    for peer in peers:
        at = pl.multiple_of((peer // 2) * BLOCK, BLOCK)
        arrived(act_ref.at[pl.ds(row, ROWS), pl.ds(at, BLOCK)], recv.at[peer // 2])
    part = act_ref.at[pl.ds(row, ROWS), :]
    copy = push(part, part, fsend, frecv, partner)
    copy.start()
    for other in copies:
        other.wait_send()
    copy.wait_send()
    other_row = pl.multiple_of((1 - core) * ROWS, ROWS)
    arrived(act_ref.at[pl.ds(other_row, ROWS), :], frecv)


def forward(x, cross, local):
    return pl.pallas_call(
        forward_kernel,
        out_shape=(
            jax.ShapeDtypeStruct((4, 4, 2, 256, 256), BF16),
            jax.ShapeDtypeStruct((4, 4, ROWS, 256), F32),
            jax.ShapeDtypeStruct((512, 1024), BF16),
        ),
        in_specs=[VMEM] * 3,
        out_specs=(VMEM, VMEM, ANY),
        scratch_shapes=[
            pltpu.VMEM((ROWS, 1024), BF16), DMA((CHIPS,)), DMA((CHIPS,)), DMA, DMA, DMA,
        ],
        compiler_params=params_of(2),
    )(x, cross, local)


ORDER = [(1, 1), (3, 1), (2, 1), (2, 0), (1, 0), (3, 0), (0, 1), (0, 0)]


def output_kernel(act_ref, cat_ref, out_ref, weights, sends, lands, wsem, send, recv):
    me = lax.axis_index("tensor")
    core = lax.rem(me, 2)
    chip = me // 2
    x_at, y_at = lax.rem(chip, 2), chip // 2
    across = 2 * (chip + 1 - 2 * x_at) + core
    up = 2 * lax.rem(chip + 2, CHIPS) + core
    down = 2 * lax.rem(chip + 6, CHIPS) + core
    fetches = []
    for k, (dy, dx) in enumerate(ORDER):
        target = 2 * lax.rem(y_at + dy, 4) + lax.rem(x_at + dx, 2)
        copy = pltpu.make_async_copy(
            cat_ref.at[:, pl.ds(pl.multiple_of(target * 512, 512), 512)], weights.at[k], wsem.at[k]
        )
        copy.start()
        fetches.append(copy)
    meet([across, up, down])
    started = []

    def product(k, half):
        if half is None:
            return dot(act_ref[...], weights[k])
        return dot(act_ref[half * ROWS:(half + 1) * ROWS], weights[k])

    def give(slot, value, peer):
        sends[slot] = value.astype(BF16)
        copy = push(sends.at[slot], lands.at[slot], send.at[slot], recv.at[slot], peer)
        copy.start()
        started.append(copy)

    def take(slot):
        arrived(lands.at[slot], recv.at[slot])
        return lands[slot].astype(F32)

    fetches[0].wait()
    fetches[1].wait()
    fetches[2].wait()
    for half in range(2):
        give(0 + half, product(0, half), up)
        give(2 + half, product(1, half), down)
        give(4 + half, product(2, half), across)
    fetches[3].wait()
    give(6, product(3, 0) + take(4), up)
    give(7, product(3, 1) + take(5), down)
    fetches[4].wait()
    fetches[5].wait()
    give(8, product(4, 1), up)
    give(9, product(5, 0), down)
    fetches[6].wait()
    for half in range(2):
        give(12 + half, product(6, half) + (take(0 + half) + take(2 + half)), across)
    give(10, product(4, 0) + take(6), up)
    give(11, product(5, 1) + take(7), down)
    fetches[7].wait()
    out_ref[0:ROWS] = product(7, 0) + (take(9) + take(12)) + take(10)
    out_ref[ROWS:] = product(7, 1) + (take(8) + take(13)) + take(11)
    for copy in started:
        copy.wait_send()


def project(act, cat):
    return pl.pallas_call(
        output_kernel,
        out_shape=jax.ShapeDtypeStruct((512, 512), F32),
        in_specs=[VMEM, ANY],
        out_specs=VMEM,
        scratch_shapes=[
            pltpu.VMEM((CHIPS, 1024, 512), BF16),
            pltpu.VMEM((14, ROWS, 512), BF16), pltpu.VMEM((14, ROWS, 512), BF16),
            DMA((CHIPS,)), DMA((14,)), DMA((14,)),
        ],
        compiler_params=params_of(3),
    )(act, cat)


def cotangent_kernel(
    grad_ref, cat_ref, rg_ref, weights, grads, mine, theirs, landed, rounded,
    wsem, gsem, psend, precv, send, recv, local,
):
    me = lax.axis_index("tensor")
    core = lax.rem(me, 2)
    chip = me // 2
    partner = me + 1 - 2 * core
    fetches = []
    for j in range(CHIPS):
        at = pl.multiple_of((2 * j + core) * 512, 512)
        one = pltpu.make_async_copy(cat_ref.at[:, pl.ds(j * 512, 512)], weights.at[j], wsem.at[j])
        two = pltpu.make_async_copy(grad_ref.at[:, pl.ds(at, 512)], grads.at[j], gsem.at[j])
        one.start()
        two.start()
        fetches.append((one, two))
    peers = [lax.rem(me + 2 * k, GROUP) for k in range(1, CHIPS)]
    meet(peers + [partner])
    other_row = pl.multiple_of((1 - core) * ROWS, ROWS)
    row = pl.multiple_of(core * ROWS, ROWS)
    for j in range(CHIPS):
        for copy in fetches[j]:
            copy.wait()
        value = dot(grads[j, pl.ds(other_row, ROWS), :], weights[j], NT)
        if j == 0:
            theirs[...] = value
        else:
            theirs[...] += value
    swap = push(theirs, landed, psend, precv, partner)
    swap.start()
    for j in range(CHIPS):
        value = dot(grads[j, pl.ds(row, ROWS), :], weights[j], NT)
        if j == 0:
            mine[...] = value
        else:
            mine[...] += value
    swap.wait()
    rounded[...] = (mine[...] + landed[...]).astype(BF16)
    column = pl.multiple_of(chip * BLOCK, BLOCK)
    landing = rg_ref.at[:, pl.ds(column, BLOCK)]
    copies = []
    for k, peer in enumerate(peers):
        source = pl.multiple_of((peer // 2) * BLOCK, BLOCK)
        copy = push(rounded.at[:, pl.ds(source, BLOCK)], landing, send.at[k], recv.at[chip], peer)
        copy.start()
        copies.append(copy)
    own = pltpu.make_async_copy(rounded.at[:, pl.ds(column, BLOCK)], landing, local)
    own.start()
    own.wait()
    for peer in peers:
        at = pl.multiple_of((peer // 2) * BLOCK, BLOCK)
        arrived(rg_ref.at[:, pl.ds(at, BLOCK)], recv.at[peer // 2])
    for copy in copies:
        copy.wait_send()


def cotangent(grads, cat):
    return pl.pallas_call(
        cotangent_kernel,
        out_shape=jax.ShapeDtypeStruct((ROWS, 1024), BF16),
        in_specs=[ANY, ANY],
        out_specs=ANY,
        scratch_shapes=[
            pltpu.VMEM((CHIPS, 1024, 512), BF16), pltpu.VMEM((CHIPS, 512, 512), BF16),
            pltpu.VMEM((ROWS, 1024), F32), pltpu.VMEM((ROWS, 1024), F32),
            pltpu.VMEM((ROWS, 1024), F32), pltpu.VMEM((ROWS, 1024), BF16),
            DMA((CHIPS,)), DMA((CHIPS,)), DMA, DMA, DMA((CHIPS,)), DMA((CHIPS,)), DMA,
        ],
        compiler_params=params_of(4),
    )(grads, cat)


def backward_kernel(
    rg_ref, x_ref, saved_ref, mats_ref, own_ref, cross, locals_, cross_in, local_in,
    send, recv, lsend, lrecv, psend, precv,
):
    me = lax.axis_index("tensor")
    core = lax.rem(me, 2)
    chip = me // 2
    partner = me + 1 - 2 * core
    meet([lax.rem(me + k, GROUP) for k in range(1, GROUP)])
    state = [rg_ref[:, index * 256:(index + 1) * 256].astype(F32) for index in range(4)]
    state = regroup(state)
    swaps = []
    for level in (3, 2, 1, 0):
        outs = []
        for index in range(4):
            grad = split(state[index])
            full = dot3(split(saved_ref[level, index]), grad, TN)
            if level % 2 == 0:
                a, b = full[:BLOCK, :BLOCK], full[BLOCK:, BLOCK:]
            else:
                a, b = take_far(full)
            one, two = pairs_of(level, index)
            cross[level, one % 2, one // 2] = a
            cross[level, two % 2, two // 2] = b
            outs.append(dot3(grad, (mats_ref[level, index, 0], mats_ref[level, index, 1]), NT))
        state = regroup(outs) if level == 2 else outs
        copy = push(
            cross.at[level, 1 - core], cross_in.at[level], psend.at[level], precv.at[level], partner
        )
        copy.start()
        swaps.append(copy)
    for m in range(CHIPS):
        grad = split(state[m // 2][:, (m % 2) * BLOCK:(m % 2 + 1) * BLOCK])
        for side in range(2):
            x = x_ref[2 * m + side]
            full = dot(grad[0], x, TN) + dot(grad[1], x, TN)
            locals_[side, m] = full[side * HALF:(side + 1) * HALF]
    copy = push(locals_.at[1 - core], local_in, psend.at[4], precv.at[4], partner)
    copy.start()
    swaps.append(copy)

    def start(src, dst, send_sem, recv_sem, peer):
        @pl.when(peer == me)
        def _():
            pltpu.make_async_copy(src, dst, recv_sem).start()

        @pl.when(peer != me)
        def _():
            push(src, dst, send_sem, recv_sem, peer).start()

    def drain(src, dst, send_sem, recv_sem, peer):
        @pl.when(peer != me)
        def _():
            push(src, dst, send_sem, recv_sem, peer).wait_send()

    jobs = []
    for level in (3, 2, 1, 0):
        swaps[3 - level].wait()
        cross_in[level] = cross_in[level] + cross[level, core]
        for q in range(4):
            peer = pair_owner(2 * q + core, level, chip // 4)
            slot = lax.rem(chip, 4)
            job = (
                cross_in.at[level, q], own_ref.at[4 + 4 * level + slot],
                send.at[level, q], recv.at[level, slot], peer,
            )
            start(*job)
            jobs.append(job)
    swaps[4].wait()
    local_in[...] = local_in[...] + locals_[core]
    for q in range(CHIPS):
        side = pl.multiple_of(lax.rem(chip, 2) * HALF, HALF)
        job = (
            local_in.at[q], own_ref.at[chip // 2, pl.ds(side, HALF), :],
            lsend.at[q], lrecv.at[chip], 2 * q + core,
        )
        start(*job)
        jobs.append(job)
    for job in jobs:
        drain(*job)
    for level in range(4):
        for c in range(4):
            arrived(own_ref.at[4 + 4 * level + c], recv.at[level, c])
    for g in range(CHIPS):
        arrived(own_ref.at[g // 2, pl.ds((g % 2) * HALF, HALF), :], lrecv.at[g])


def backward(rg, x, saved, mats):
    return pl.pallas_call(
        backward_kernel,
        out_shape=jax.ShapeDtypeStruct((20, BLOCK, BLOCK), F32),
        in_specs=[VMEM] * 4,
        out_specs=ANY,
        scratch_shapes=[
            pltpu.VMEM((4, 2, 4, BLOCK, BLOCK), F32), pltpu.VMEM((2, CHIPS, HALF, BLOCK), F32),
            pltpu.VMEM((4, 4, BLOCK, BLOCK), F32), pltpu.VMEM((CHIPS, HALF, BLOCK), F32),
            DMA((4, 4)), DMA((4, 4)), DMA((CHIPS,)), DMA((CHIPS,)), DMA((5,)), DMA((5,)),
        ],
        compiler_params=params_of(5),
    )(rg, x, saved, mats)


def pull_many(inverse, matrix_grad):
    highest = lax.Precision.HIGHEST
    left = jnp.einsum("nji,njk->nik", inverse, matrix_grad, precision=highest)
    full = jnp.einsum("nik,njk->nij", left, inverse, precision=highest)
    return -2.0 * (full - full.transpose(0, 2, 1))


def body(tokens, frozen, local_param, cross_param, out_grad):
    gathered = lax.all_gather(out_grad, "tensor", axis=1, tiled=True)
    x, cat = spread(tokens, frozen)
    cat = cat.reshape(1024, 4096)
    params = jnp.concatenate([local_param, cross_param.reshape(-1, BLOCK, BLOCK)])
    inverse, rotations = inverse_many(params)
    cross, local = route(rotations)
    mats, saved, act = forward(x, cross, local)
    output = project(act, cat)
    rg = cotangent(gathered, cat)
    matrix_grad = backward(rg, x, saved, mats)
    matrix_grad = lax.psum(matrix_grad, "dp")
    matrix_grad = jnp.concatenate([matrix_grad[:4].transpose(0, 2, 1), matrix_grad[4:]])
    grads = pull_many(inverse, matrix_grad)
    return output, grads[:4], grads[4:].reshape(4, 4, BLOCK, BLOCK)


def solution(mesh):
    in_specs = (
        P("dp", "tensor"),
        P("tensor", None),
        P("tensor", None, None),
        P(None, "tensor", None, None),
        P("dp", "tensor"),
    )
    out_specs = (P("dp", "tensor"), P("tensor", None, None), P(None, "tensor", None, None))
    return jax.shard_map(body, mesh=mesh, in_specs=in_specs, out_specs=out_specs, check_vma=False)
```

time: 791 us -> 397 us (0.50); the launches traced: 777 us -> 392 us
  waiting for transfers between devices: 303 us -> 56.8 us
  local copies, waits for them, and re-layouts: 80.2 us -> 6.42 us
  Pallas kernels: 247 us -> 308 us
  other arithmetic: 56.5 us -> 1.54 us
  matrix products: 57.4 us -> 5.11 us
  starting transfers between devices: 18.5 us -> 0.08 us
    reduce_scatter x1 -> x0, waiting for transfers between devices: 173 us -> none  [body(): lax.psum_scatter(partial_out, 'tensor', scatter_dimension=1, tiled=True)]
    pallas_call x1 -> x7, Pallas kernels: 247 us -> 308 us  [the longest x1 136 us: spread(): pl.pallas_call(spread_kernel, out_shape=(jax.ShapeDtypeStruct((GROUP, ROW...]
    dot_general x16 -> x0, matrix products: 51 us -> none  [the longest x4 14.3 us: body(): jnp.einsum('tci,tcj->cij', saved[level_idx], grad_vector, precision=highest)]
    ppermute x16 -> x0, waiting for transfers between devices: 50 us -> none  [from_partner(): lax.ppermute(shard, axis, [(i, i ^ 1 << stride) for i in range(lax.axis_s...]
    select_n x24 -> x0, other arithmetic: 48.1 us -> none  [the longest x8 25.1 us: split_halves(): other_part = jnp.where(upper_side, halves[:, 0], halves[:, 1])]
    ppermute x16 -> x0, local copies, waits for them, and re-layouts: 31.5 us -> none  [from_partner(): lax.ppermute(shard, axis, [(i, i ^ 1 << stride) for i in range(lax.axis_s...]
    select_n x16 -> x0, local copies, waits for them, and re-layouts: 28.7 us -> none  [the longest x8 15 us: split_halves(): other_part = jnp.where(upper_side, halves[:, 0], halves[:, 1])]
    psum x1, waiting for transfers between devices: 79.3 us -> 56 us  [body(): matrix_grad = lax.psum(matrix_grad, 'dp')]
  transfers between devices with their start and end apart: 19 -> 2, of which waited for: 11 -> 1; matrix products, arithmetic and copies ran while one was open for 17% -> 0% of each run, Pallas kernels for 32% -> 67%
where the time goes in v2:
time: 397 us; the launch traced here: 392 us
  Pallas kernels  308 us (78%)
  waiting for transfers between devices  56.8 us (14%)
  between operations  14.2 us (4%)
  local copies, waits for them, and re-layouts  6.42 us (2%)
  matrix products  5.11 us (1%)
    pallas_call x1, Pallas kernels, spread(): pl.pallas_call(spread_kernel, out_shape=(jax.ShapeDtypeStruct((GROUP, ROW...  136 us
    psum x1, waiting for transfers between devices, body(): matrix_grad = lax.psum(matrix_grad, 'dp')  56 us
    pallas_call x1, Pallas kernels, project(): pl.pallas_call(output_kernel, out_shape=jax.ShapeDtypeStruct((512, 512),...  50.3 us
    pallas_call x1, Pallas kernels, route(): pl.pallas_call(route_kernel, out_shape=(jax.ShapeDtypeStruct((4, 4, 2, BL...  31.9 us
    pallas_call x1, Pallas kernels, backward(): pl.pallas_call(backward_kernel, out_shape=jax.ShapeDtypeStruct((20, BLOCK...  29.5 us
    pallas_call x1, Pallas kernels, inverse_many(): pl.pallas_call(inverse_kernel, out_shape=(shape, shape), compiler_params=...  23.2 us
    pallas_call x1, Pallas kernels, forward(): pl.pallas_call(forward_kernel, out_shape=(jax.ShapeDtypeStruct((4, 4, 2,...  20.6 us
    pallas_call x1, Pallas kernels, cotangent(): pl.pallas_call(cotangent_kernel, out_shape=jax.ShapeDtypeStruct((ROWS, 10...  16.7 us
  transfers between devices with their start and end apart: 2, of which 1 were waited for; matrix products, arithmetic and copies ran while one was open for 0% of the time, Pallas kernels for 67%

profile of v2, /device:TPU:6, one launch (start us, length us, event | category | flops | bytes accessed | tf_op | source)
XLA Modules:
  0.0 392.4 jit_solution(4157693298547417810)
XLA Ops:
  7.2 0.0 all-gather.2.cloned.1.call-start
  7.2 0.7 all-gather.2.cloned.1.call-update
  7.9 0.0 all-reduce.2.cloned.1.call-start
  7.9 1.4 pad_maximum_fusion.param_ref
  9.3 23.2 %shard_map.77 = (f32[20,128,128]{2,1,0:T(8,128)S(1)}, f32[20,128,128]{2,1,0:T(8,128)S(1)}) custom-call(f32[20,128,128]{2,1,0:T(8,128)S(1)} %pad_maximum_fusion.param_ref), custom_call_target="tpu_custom_call" | custom-call | tf_op jit(solution)/shard_map/pallas_call | solution.py:171
  32.6 1.1 copy-done
  33.6 31.9 %shard_map.78 = (f32[4,4,2,128,128]{4,3,2,1,0:T(8,128)}, f32[8,2,64,128]{3,2,1,0:T(8,128)}) custom-call(f32[20,128,128]{2,1,0:T(8,128)} %copy-done), custom_call_target="tpu_custom_call" | custom-call | tf_op jit(solution)/shard_map/pallas_call | solution.py:253
  65.6 136.1 %shard_map.76 = (bf16[16,256,128]{2,1,0:T(8,128)(2,1)}, bf16[8,2,64,4096]{3,2,1,0:T(8,128)(2,1)}) custom-call(bf16[512,512]{1,0:T(8,128)(2,1)} %tok_ref.1, bf16[8,64,8192]{2,1,0:T(8,128)(2,1)} %bitcast.14), custom_call_target="tpu_custom_call" | custom-call | tf_op jit(solution)/shard_map/pallas_call | solution.py:112
  201.7 20.6 %shard_map.79 = (bf16[4,4,2,256,256]{4,3,2,1,0:T(8,128)(2,1)}, f32[4,4,256,256]{3,2,1,0:T(8,128)}, bf16[512,1024]{1,0:T(8,128)(2,1)}) custom-call(bf16[16,256,128]{2,1,0:T(8,128)(2,1)} %get-tuple-element.12.x_ref, f32[4,4,2,128,128]{4,3,2,1,0:T(8,128)} %get-tuple-element.14.cross_ref, f32[8,2,64,128]{3,2,1,0:T(8,128)} %get-tuple-element.15.local_ref), custom_call_target="tpu_custom_call" | custom-call | tf_op jit(solution)/shard_map/pallas_call | solution.py:384
  222.3 0.0 all-gather.2.cloned.1.call-done.grad_ref
  222.3 16.7 %shard_map.81.rg_ref = bf16[256,1024]{1,0:T(8,128)(2,1)} custom-call(bf16[512,8192]{1,0:T(8,128)(2,1)} %all-gather.2.cloned.1.call-done.grad_ref, bf16[1024,4096]{1,0:T(8,128)(2,1)} %bitcast.12), custom_call_target="tpu_custom_call" | custom-call | tf_op jit(solution)/shard_map/pallas_call | solution.py:535
  239.1 29.5 %shard_map.82 = f32[20,128,128]{2,1,0:T(8,128)} custom-call(bf16[256,1024]{1,0:T(8,128)(2,1)} %shard_map.81.rg_ref, bf16[16,256,128]{2,1,0:T(8,128)(2,1)} %get-tuple-element.12.x_ref, f32[4,4,256,256]{3,2,1,0:T(8,128)} %get-tuple-element.19.saved_ref, bf16[4,4,2,256,256]{4,3,2,1,0:T(8,128)(2,1)} %get-tuple-element.20.mats_ref), custom_call_target="tpu_custom_call" | custom-call | tf_op jit(solution)/shard_map/pallas_call | solution.py:638
  268.6 50.3 %shard_map.80 = f32[512,512]{1,0:T(8,128)} custom-call(bf16[512,1024]{1,0:T(8,128)(2,1)} %get-tuple-element.16.act_ref, bf16[1024,4096]{1,0:T(8,128)(2,1)} %bitcast.13), custom_call_target="tpu_custom_call" | custom-call | tf_op jit(solution)/shard_map/pallas_call | solution.py:464
  318.9 56.0 %all-reduce.2.cloned.1.call-done = f32[20,128,128]{2,1,0:T(8,128)} async-done(((f32[20,128,128]{2,1,0:T(8,128)}), f32[20,128,128]{2,1,0:T(8,128)}) %all-reduce.2.cloned.1.call-update) | async-done | bytes 1310736 | tf_op jit(solution)/shard_map/psum | solution.py:670
  374.9 1.0 slice.16
  375.9 0.1 copy.10
  376.1 1.1 slice-done
  377.1 2.3 fusion
  379.4 2.8 fusion.6
  382.3 0.4 copy.9
  382.7 0.2 fusion.4
  382.8 0.7 slice.18
  383.6 1.1 slice.19
  384.6 1.0 copy.13
  (5 shorter events, 0.0 us)
Async XLA Ops:
  7.2 215.2 %all-gather.2.cloned.1.call-start = ((), (), s32[]{:S(2)}) async-start(), calls=%async_computation | async-start | bytes 8912896 | tf_op jit(solution)/shard_map/all_gather | solution.py:660
  7.9 367.0 %all-reduce.2.cloned.1.call-start = ((), (), s32[]{:S(2)}) async-start(), calls=%async_computation.1 | async-start | bytes 2621440 | tf_op jit(solution)/shard_map/psum | solution.py:670
  32.6 1.1 copy-start
  375.9 1.2 slice-start
  382.8 1.8 copy-start.1
Sparse Core Ops, SparseCore 0:
  9.7 77.4 all-gather.1
  268.7 106.1 all-reduce.1

commit v3 on v2

v3 whole, which is shorter than its diff:
```python
import functools

import jax
import jax.numpy as jnp
from jax import lax
from jax.experimental import pallas as pl
from jax.experimental.pallas import tpu as pltpu
from jax.sharding import PartitionSpec as P

MESH = pl.DeviceIdType.MESH
F32 = jnp.float32
BF16 = jnp.bfloat16
ANY = pl.BlockSpec(memory_space=pl.ANY)
VMEM = pl.BlockSpec(memory_space=pltpu.VMEM)
DMA = pltpu.SemaphoreType.DMA
GROUP = 16
CHIPS = 8
HALF = 64
BLOCK = 128
ROWS = 256


def params_of(identity, vmem=60):
    return pltpu.CompilerParams(
        collective_id=identity, has_side_effects=True, vmem_limit_bytes=vmem << 20
    )


def meet(peers, axis="tensor"):
    barrier = pltpu.get_barrier_semaphore()
    for peer in peers:
        pl.semaphore_signal(barrier, inc=1, device_id={axis: peer}, device_id_type=MESH)
    pl.semaphore_wait(barrier, len(peers))


def push(src, dst, send, recv, peer, axis="tensor"):
    return pltpu.make_async_remote_copy(
        src_ref=src, dst_ref=dst, send_sem=send, recv_sem=recv,
        device_id={axis: peer}, device_id_type=MESH,
    )


def start_job(src, dst, send, recv, peer, me):
    @pl.when(peer == me)
    def _():
        pltpu.make_async_copy(src, dst, recv).start()

    @pl.when(peer != me)
    def _():
        push(src, dst, send, recv, peer).start()


def drain_job(src, dst, send, recv, peer, me):
    @pl.when(peer != me)
    def _():
        push(src, dst, send, recv, peer).wait_send()


def arrived(ref, sem):
    pltpu.make_async_copy(ref, ref, sem).wait()


def split(value):
    high = value.astype(BF16)
    return high, (value - high.astype(F32)).astype(BF16)


def dot(a, b, dims=(((1,), (0,)), ((), ()))):
    return lax.dot_general(a, b, dims, preferred_element_type=F32)


NT = (((1,), (1,)), ((), ()))
TN = (((0,), (0,)), ((), ()))


def dot3(a, b, dims=(((1,), (0,)), ((), ()))):
    return dot(a[0], b[0], dims) + (dot(a[0], b[1], dims) + dot(a[1], b[0], dims))


def inverse_blocks(param_ref, out_ref, rot_ref):
    count, size, _ = param_ref.shape
    step = 32
    rows = lax.broadcasted_iota(jnp.int32, (size, size), 0)
    lanes = lax.broadcasted_iota(jnp.int32, (size, size), 1)
    panel_rows = lax.broadcasted_iota(jnp.int32, (step, size), 0)
    panel_lanes = lax.broadcasted_iota(jnp.int32, (step, size), 1)
    identity = jnp.where(rows == lanes, 1.0, 0.0)
    for at in range(count):
        param = param_ref[at]
        out_ref[at] = identity + param - param.T

    def eliminate(block_at, carry):
        start = pl.multiple_of(block_at * step, step)
        shift = lax.rem(size - start, size)
        inside = (lanes >= start) & (lanes < start + step)
        panels = [pltpu.roll(out_ref[at, pl.ds(start, step), :], shift, 1) for at in range(count)]
        for k in range(step):
            for at in range(count):
                panel = panels[at]
                column = panel[:, k:k + 1]
                scale = 1.0 / panel[k:k + 1, k:k + 1]
                row = jnp.where(panel_lanes[:1] == k, 1.0, panel[k:k + 1, :]) * scale
                rest = jnp.where(panel_lanes == k, 0.0, panel) - column * row
                panels[at] = jnp.where(panel_rows == k, row, rest)
        panels = [pltpu.roll(panel, start, 1) for panel in panels]
        for at in range(count):
            matrix = out_ref[at]
            turned = pltpu.roll(matrix, shift, 1)[:, :step]
            out_ref[at] = jnp.where(inside, 0.0, matrix) - jnp.dot(
                turned, panels[at], precision=lax.Precision.HIGHEST, preferred_element_type=F32
            )
        for at in range(count):
            out_ref[at, pl.ds(start, step), :] = panels[at]
        return carry

    lax.fori_loop(0, size // step, eliminate, 0)
    for at in range(count):
        rotation = 2.0 * out_ref[at] - identity
        rot_ref[at] = rotation.T if at < 4 else rotation


def pair_place(me, level):
    low = 2 ** level
    bit = lax.rem(me // low, 2)
    pair = (me // (2 * low)) * low + lax.rem(me, low)
    return bit, pair


def pair_owner(pair, level, bit):
    low = 2 ** level
    return (pair // low) * (2 * low) + bit * low + lax.rem(pair, low)


def mix(a, b, r):
    at = (r // 2) * BLOCK
    first, second = a[:, at:at + BLOCK], b[:, at:at + BLOCK]
    lanes = lax.broadcasted_iota(jnp.int32, first.shape, 1)
    if r % 2 == 0:
        return jnp.where(lanes < HALF, first, pltpu.roll(second, HALF, 1))
    return jnp.where(lanes < HALF, pltpu.roll(first, HALF, 1), second)


def regroup(quads):
    return [
        jnp.concatenate([mix(quads[0], quads[1], r), mix(quads[2], quads[3], r)], axis=1)
        for r in range(4)
    ]


def place_near(a, b):
    zero = jnp.zeros((BLOCK, BLOCK), F32)
    return jnp.concatenate(
        [jnp.concatenate([a, zero], axis=1), jnp.concatenate([zero, b], axis=1)], axis=0
    )


def place_far(a, b):
    lanes = lax.broadcasted_iota(jnp.int32, (BLOCK, BLOCK), 1)
    turned_a, turned_b = pltpu.roll(a, HALF, 1), pltpu.roll(b, HALF, 1)
    low = lanes < HALF
    a_rows = jnp.concatenate([jnp.where(low, a, 0.0), jnp.where(low, turned_a, 0.0)], axis=1)
    b_rows = jnp.concatenate([jnp.where(low, 0.0, turned_b), jnp.where(low, 0.0, b)], axis=1)
    return jnp.concatenate(
        [a_rows[:HALF], b_rows[:HALF], a_rows[HALF:], b_rows[HALF:]], axis=0
    )


def take_far(full):
    lanes = lax.broadcasted_iota(jnp.int32, (BLOCK, BLOCK), 1)
    low = lanes < HALF
    a_rows = jnp.concatenate([full[:HALF], full[BLOCK:BLOCK + HALF]], axis=0)
    b_rows = jnp.concatenate([full[HALF:BLOCK], full[BLOCK + HALF:]], axis=0)
    a = jnp.where(low, a_rows[:, :BLOCK], pltpu.roll(a_rows[:, BLOCK:], HALF, 1))
    b = jnp.where(low, pltpu.roll(b_rows[:, :BLOCK], HALF, 1), b_rows[:, BLOCK:])
    return a, b


def pairs_of(level, index):
    if level < 2:
        return 2 * index, 2 * index + 1
    return index, 4 + index


def start_kernel(
    tok_ref, froz_ref, param_ref,
    x_ref, cat_ref, inv_ref, mats_ref, saved_ref, act_ref,
    x_scr, rot, cross, local, mats, saved, rotated,
    tsend, trecv, fsend, frecv, send, recv, lsend, lrecv, psend, precv, asend, arecv, wsem,
):
    me = lax.axis_index("tensor")
    core = lax.rem(me, 2)
    chip = me // 2
    partner = me + 1 - 2 * core
    others = [lax.rem(me + k, GROUP) for k in range(1, GROUP)]
    meet(others)

    def token_slice(peer):
        column = pl.multiple_of((peer // 4) * BLOCK, BLOCK)
        row = pl.multiple_of(lax.rem(peer, 2) * ROWS, ROWS)
        return tok_ref.at[pl.ds(row, ROWS), pl.ds(column, BLOCK)]

    sends = []
    for k, peer in enumerate(others):
        copy = push(token_slice(peer), x_scr.at[me], tsend.at[k], trecv.at[me], peer)
        copy.start()
        sends.append(copy)
    pltpu.make_async_copy(token_slice(me), x_scr.at[me], trecv.at[me]).start()
    for j in range(CHIPS):
        theirs = pl.multiple_of((2 * j + 1 - core) * 512, 512)
        target = cat_ref.at[:, :, pl.ds(j * 512, 512)]
        copy = push(froz_ref.at[:, :, pl.ds(theirs, 512)], target, fsend.at[j], frecv.at[j], partner)
        copy.start()
        sends.append(copy)

    inverse_blocks(param_ref, inv_ref, rot)

    jobs = []
    for k in range(4):
        c = lax.rem(chip + k, 4)
        for side in range(2):
            jobs.append((
                rot.at[c, pl.ds(side * HALF, HALF), :], local.at[chip, core],
                lsend.at[k, side], lrecv.at[chip], 2 * (2 * c + side) + core, me,
            ))
    for level in range(4):
        bit, pair = pair_place(me, level)
        for k in range(4):
            c = lax.rem(chip + k, 4)
            jobs.append((
                rot.at[4 + 4 * level + c], cross.at[level, pair // 2, lax.rem(pair, 2)],
                send.at[level, k], recv.at[level, pair // 2],
                2 * (c + 4 * bit) + lax.rem(pair, 2), me,
            ))
    for job in jobs:
        start_job(*job)
    writes = []

    def forward_on(stage):
        if stage == 0:
            for q in range(CHIPS):
                arrived(local.at[q, core], lrecv.at[q])
            part = local.at[:, core]
        else:
            for q in range(4):
                arrived(cross.at[stage - 1, q, core], recv.at[stage - 1, q])
            part = cross.at[stage - 1, :, core]
        copy = push(part, part, psend.at[stage], precv.at[stage], partner)
        copy.start()
        sends.append(copy)

    forward_on(0)
    forward_on(1)
    for peer in [me] + others:
        arrived(x_scr.at[peer], trecv.at[peer])
    copy = pltpu.make_async_copy(x_scr, x_ref, wsem.at[0])
    copy.start()
    writes.append(copy)
    arrived(local.at[:, 1 - core], precv.at[0])
    lanes = lax.broadcasted_iota(jnp.int32, (ROWS, BLOCK), 1)
    for m in range(CHIPS):
        parts = []
        for side in range(2):
            high, low = split(jnp.concatenate([local[m, side]] * 2, axis=0))
            x = x_scr[2 * m + side]
            parts.append(dot(x, high, NT) + dot(x, low, NT))
        saved[0, m // 2, :, (m % 2) * BLOCK:(m % 2 + 1) * BLOCK] = jnp.where(
            lanes < HALF, parts[0], parts[1]
        )
    for level in range(4):
        if level < 3:
            forward_on(level + 2)
        copy = pltpu.make_async_copy(saved.at[level], saved_ref.at[level], wsem.at[1 + level])
        copy.start()
        writes.append(copy)
        arrived(cross.at[level, :, 1 - core], precv.at[level + 1])
        outs = []
        for index in range(4):
            one, two = pairs_of(level, index)
            a = cross[level, one // 2, one % 2]
            b = cross[level, two // 2, two % 2]
            matrix = split(place_near(a, b) if level % 2 == 0 else place_far(a, b))
            mats[level, index, 0] = matrix[0]
            mats[level, index, 1] = matrix[1]
            outs.append(dot3(split(saved[level, index]), matrix))
        copy = pltpu.make_async_copy(mats.at[level], mats_ref.at[level], wsem.at[5 + level])
        copy.start()
        writes.append(copy)
        if level % 2 == 1:
            outs = regroup(outs)
        for index in range(4):
            if level < 3:
                saved[level + 1, index] = outs[index]
            else:
                rotated[:, index * 256:(index + 1) * 256] = outs[index].astype(BF16)
    row = pl.multiple_of(core * ROWS, ROWS)
    column = pl.multiple_of(chip * BLOCK, BLOCK)
    landing = act_ref.at[pl.ds(row, ROWS), pl.ds(column, BLOCK)]
    peers = [lax.rem(me + 2 * k, GROUP) for k in range(1, CHIPS)]
    for k, peer in enumerate(peers):
        source = pl.multiple_of((peer // 2) * BLOCK, BLOCK)
        copy = push(rotated.at[:, pl.ds(source, BLOCK)], landing, asend.at[k], arecv.at[chip], peer)
        copy.start()
        sends.append(copy)
    pltpu.make_async_copy(rotated.at[:, pl.ds(column, BLOCK)], landing, arecv.at[chip]).start()
    for peer in [me] + peers:
        at = pl.multiple_of((peer // 2) * BLOCK, BLOCK)
        arrived(act_ref.at[pl.ds(row, ROWS), pl.ds(at, BLOCK)], arecv.at[peer // 2])
    part = act_ref.at[pl.ds(row, ROWS), :]
    copy = push(part, part, psend.at[5], precv.at[5], partner)
    copy.start()
    sends.append(copy)
    for copy in writes:
        copy.wait()
    for copy in sends:
        copy.wait_send()
    for job in jobs:
        drain_job(*job)
    for j in range(CHIPS):
        arrived(cat_ref.at[:, :, pl.ds(j * 512, 512)], frecv.at[j])
    other_row = pl.multiple_of((1 - core) * ROWS, ROWS)
    arrived(act_ref.at[pl.ds(other_row, ROWS), :], precv.at[5])


def start(tokens, frozen, params):
    return pl.pallas_call(
        start_kernel,
        out_shape=(
            jax.ShapeDtypeStruct((GROUP, ROWS, BLOCK), BF16),
            jax.ShapeDtypeStruct((CHIPS, HALF, 4096), BF16),
            jax.ShapeDtypeStruct((20, BLOCK, BLOCK), F32),
            jax.ShapeDtypeStruct((4, 4, 2, 256, 256), BF16),
            jax.ShapeDtypeStruct((4, 4, ROWS, 256), F32),
            jax.ShapeDtypeStruct((512, 1024), BF16),
        ),
        in_specs=[ANY, ANY, VMEM],
        out_specs=(ANY, ANY, VMEM, ANY, ANY, ANY),
        scratch_shapes=[
            pltpu.VMEM((GROUP, ROWS, BLOCK), BF16), pltpu.VMEM((20, BLOCK, BLOCK), F32),
            pltpu.VMEM((4, 4, 2, BLOCK, BLOCK), F32), pltpu.VMEM((CHIPS, 2, HALF, BLOCK), F32),
            pltpu.VMEM((4, 4, 2, 256, 256), BF16), pltpu.VMEM((4, 4, ROWS, 256), F32),
            pltpu.VMEM((ROWS, 1024), BF16),
            DMA((GROUP,)), DMA((GROUP,)), DMA((CHIPS,)), DMA((CHIPS,)),
            DMA((4, 4)), DMA((4, 4)), DMA((4, 2)), DMA((CHIPS,)), DMA((6,)), DMA((6,)),
            DMA((CHIPS,)), DMA((CHIPS,)), DMA((9,)),
        ],
        compiler_params=params_of(0),
    )(tokens, frozen.reshape(CHIPS, HALF, 8192), params)


ORDER = [(1, 1), (3, 1), (2, 1), (2, 0), (1, 0), (3, 0), (0, 1), (0, 0)]


def finish_kernel(
    act_hbm, froz_ref, cat_ref, grad_ref, x_hbm, saved_hbm, mats_hbm,
    out_ref, own_ref,
    act, weights, grads, x_ref, saved, mats, sends, lands, mine, theirs, landed, rounded, rg,
    cross, locals_, cross_in, local_in,
    wsem, gsem, hsem, send, recv, psend, precv, rsend, rrecv, msend, mrecv, lsend, lrecv,
):
    me = lax.axis_index("tensor")
    core = lax.rem(me, 2)
    chip = me // 2
    partner = me + 1 - 2 * core
    x_at, y_at = lax.rem(chip, 2), chip // 2
    across = 2 * (chip + 1 - 2 * x_at) + core
    up = 2 * lax.rem(chip + 2, CHIPS) + core
    down = 2 * lax.rem(chip + 6, CHIPS) + core
    load = pltpu.make_async_copy(act_hbm, act, hsem.at[0])
    load.start()
    fetches = []
    for k, (dy, dx) in enumerate(ORDER):
        target = 2 * lax.rem(y_at + dy, 4) + lax.rem(x_at + dx, 2)
        at = pl.multiple_of((2 * target + core) * 512, 512)
        one = pltpu.make_async_copy(
            froz_ref.at[:, :, pl.ds(at, 512)], weights.at[k, :, core], wsem.at[k, 0]
        )
        two = pltpu.make_async_copy(
            cat_ref.at[:, :, pl.ds(pl.multiple_of(target * 512, 512), 512)],
            weights.at[k, :, 1 - core], wsem.at[k, 1],
        )
        one.start()
        two.start()
        fetches.append((one, two))
    gets = []
    for k, (dy, dx) in enumerate(ORDER):
        target = 2 * lax.rem(y_at + dy, 4) + lax.rem(x_at + dx, 2)
        at = pl.multiple_of((2 * target + core) * 512, 512)
        copy = pltpu.make_async_copy(grad_ref.at[:, pl.ds(at, 512)], grads.at[k], gsem.at[k])
        copy.start()
        gets.append(copy)
    later = []
    for level in (3, 2, 1, 0):
        one = pltpu.make_async_copy(saved_hbm.at[level], saved.at[level], hsem.at[1 + level])
        two = pltpu.make_async_copy(mats_hbm.at[level], mats.at[level], hsem.at[5 + level])
        one.start()
        two.start()
        later.append((one, two))
    x_get = pltpu.make_async_copy(x_hbm, x_ref, hsem.at[9])
    x_get.start()
    meet([lax.rem(me + k, GROUP) for k in range(1, GROUP)])
    started = []

    def product(k, half):
        return dot(act[half * ROWS:(half + 1) * ROWS], weights[k].reshape(1024, 512))

    def fetched(k):
        for copy in fetches[k]:
            copy.wait()

    def give(slot, value, peer):
        sends[slot] = value.astype(BF16)
        copy = push(sends.at[slot], lands.at[slot], send.at[slot], recv.at[slot], peer)
        copy.start()
        started.append(copy)

    def take(slot):
        arrived(lands.at[slot], recv.at[slot])
        return lands[slot].astype(F32)

    load.wait()
    for half in range(2):
        for k, peer in ((0, up), (1, down), (2, across)):
            if half == 0:
                fetched(k)
            give(2 * k + half, product(k, half), peer)
    fetched(3)
    fetched(4)
    fetched(5)
    give(8, product(4, 1), up)
    give(9, product(5, 0), down)
    fetched(6)
    fetched(7)
    for copy in gets:
        copy.wait()
    other_row = pl.multiple_of((1 - core) * ROWS, ROWS)
    row = pl.multiple_of(core * ROWS, ROWS)
    for k in range(CHIPS):
        value = dot(grads[k, pl.ds(other_row, ROWS), :], weights[k].reshape(1024, 512), NT)
        if k == 0:
            theirs[...] = value
        else:
            theirs[...] += value
    swap = push(theirs, landed, psend.at[5], precv.at[5], partner)
    swap.start()
    give(6, product(3, 0) + take(4), up)
    give(7, product(3, 1) + take(5), down)
    for k in range(CHIPS):
        value = dot(grads[k, pl.ds(row, ROWS), :], weights[k].reshape(1024, 512), NT)
        if k == 0:
            mine[...] = value
        else:
            mine[...] += value
    swap.wait()
    rounded[...] = (mine[...] + landed[...]).astype(BF16)
    column = pl.multiple_of(chip * BLOCK, BLOCK)
    landing = rg.at[:, pl.ds(column, BLOCK)]
    peers = [lax.rem(me + 2 * k, GROUP) for k in range(1, CHIPS)]
    for k, peer in enumerate(peers):
        source = pl.multiple_of((peer // 2) * BLOCK, BLOCK)
        copy = push(rounded.at[:, pl.ds(source, BLOCK)], landing, rsend.at[k], rrecv.at[chip], peer)
        copy.start()
        started.append(copy)
    pltpu.make_async_copy(rounded.at[:, pl.ds(column, BLOCK)], landing, rrecv.at[chip]).start()
    for half in range(2):
        give(12 + half, product(6, half) + (take(0 + half) + take(2 + half)), across)
    give(10, product(4, 0) + take(6), up)
    give(11, product(5, 1) + take(7), down)
    for peer in [me] + peers:
        at = pl.multiple_of((peer // 2) * BLOCK, BLOCK)
        arrived(rg.at[:, pl.ds(at, BLOCK)], rrecv.at[peer // 2])

    state = [rg[:, index * 256:(index + 1) * 256].astype(F32) for index in range(4)]
    state = regroup(state)
    swaps = []
    for level in (3, 2, 1, 0):
        for copy in later[3 - level]:
            copy.wait()
        outs = []
        for index in range(4):
            grad = split(state[index])
            full = dot3(split(saved[level, index]), grad, TN)
            if level % 2 == 0:
                a, b = full[:BLOCK, :BLOCK], full[BLOCK:, BLOCK:]
            else:
                a, b = take_far(full)
            one, two = pairs_of(level, index)
            cross[level, one % 2, one // 2] = a
            cross[level, two % 2, two // 2] = b
            outs.append(dot3(grad, (mats[level, index, 0], mats[level, index, 1]), NT))
        state = regroup(outs) if level == 2 else outs
        copy = push(
            cross.at[level, 1 - core], cross_in.at[level], psend.at[level], precv.at[level], partner
        )
        copy.start()
        swaps.append(copy)
    x_get.wait()
    for m in range(CHIPS):
        grad = split(state[m // 2][:, (m % 2) * BLOCK:(m % 2 + 1) * BLOCK])
        for side in range(2):
            x = x_ref[2 * m + side]
            full = dot(grad[0], x, TN) + dot(grad[1], x, TN)
            locals_[side, m] = full[side * HALF:(side + 1) * HALF]
    copy = push(locals_.at[1 - core], local_in, psend.at[4], precv.at[4], partner)
    copy.start()
    swaps.append(copy)

    jobs = []
    for level in (3, 2, 1, 0):
        swaps[3 - level].wait()
        cross_in[level] = cross_in[level] + cross[level, core]
        slot = lax.rem(chip, 4)
        for k in range(4):
            q = lax.rem(chip + k, 4)
            job = (
                cross_in.at[level, q], own_ref.at[4 + 4 * level + slot],
                msend.at[level, k], mrecv.at[level, slot],
                pair_owner(2 * q + core, level, chip // 4), me,
            )
            start_job(*job)
            jobs.append(job)
    swaps[4].wait()
    local_in[...] = local_in[...] + locals_[core]
    for k in range(CHIPS):
        q = lax.rem(chip + k, CHIPS)
        side = pl.multiple_of(lax.rem(chip, 2) * HALF, HALF)
        job = (
            local_in.at[q], own_ref.at[chip // 2, pl.ds(side, HALF), :],
            lsend.at[k], lrecv.at[chip], 2 * q + core, me,
        )
        start_job(*job)
        jobs.append(job)
    out_ref[0:ROWS] = product(7, 0) + (take(9) + take(12)) + take(10)
    out_ref[ROWS:] = product(7, 1) + (take(8) + take(13)) + take(11)
    for copy in started:
        copy.wait_send()
    for job in jobs:
        drain_job(*job)
    for level in range(4):
        for c in range(4):
            arrived(own_ref.at[4 + 4 * level + c], mrecv.at[level, c])
    for g in range(CHIPS):
        arrived(own_ref.at[g // 2, pl.ds((g % 2) * HALF, HALF), :], lrecv.at[g])


def finish(act, frozen, cat, grads, x, saved, mats):
    return pl.pallas_call(
        finish_kernel,
        out_shape=(
            jax.ShapeDtypeStruct((512, 512), F32), jax.ShapeDtypeStruct((20, BLOCK, BLOCK), F32),
        ),
        in_specs=[ANY] * 7,
        out_specs=(VMEM, ANY),
        scratch_shapes=[
            pltpu.VMEM((512, 1024), BF16), pltpu.VMEM((CHIPS, CHIPS, 2, HALF, 512), BF16),
            pltpu.VMEM((CHIPS, 512, 512), BF16), pltpu.VMEM((GROUP, ROWS, BLOCK), BF16),
            pltpu.VMEM((4, 4, ROWS, 256), F32), pltpu.VMEM((4, 4, 2, 256, 256), BF16),
            pltpu.VMEM((14, ROWS, 512), BF16), pltpu.VMEM((14, ROWS, 512), BF16),
            pltpu.VMEM((ROWS, 1024), F32), pltpu.VMEM((ROWS, 1024), F32),
            pltpu.VMEM((ROWS, 1024), F32), pltpu.VMEM((ROWS, 1024), BF16),
            pltpu.VMEM((ROWS, 1024), BF16),
            pltpu.VMEM((4, 2, 4, BLOCK, BLOCK), F32), pltpu.VMEM((2, CHIPS, HALF, BLOCK), F32),
            pltpu.VMEM((4, 4, BLOCK, BLOCK), F32), pltpu.VMEM((CHIPS, HALF, BLOCK), F32),
            DMA((CHIPS, 2)), DMA((CHIPS,)), DMA((10,)), DMA((14,)), DMA((14,)), DMA((6,)), DMA((6,)),
            DMA((CHIPS,)), DMA((CHIPS,)), DMA((4, 4)), DMA((4, 4)), DMA((CHIPS,)), DMA((CHIPS,)),
        ],
        compiler_params=params_of(1),
    )(act, frozen.reshape(CHIPS, HALF, 8192), cat, grads, x, saved, mats)


def total_kernel(own_ref, out_ref, landed, part, send, recv, gsend, grecv):
    me = lax.axis_index("dp")
    others = [lax.rem(me + k, 8) for k in range(1, 8)]
    meet(others, "dp")
    copies = []
    for k, peer in enumerate(others):
        rows = own_ref.at[:, pl.ds(pl.multiple_of(peer * 16, 16), 16), :]
        copy = push(rows, landed.at[me], send.at[k], recv.at[me], peer, "dp")
        copy.start()
        copies.append(copy)
    mine = pl.ds(pl.multiple_of(me * 16, 16), 16)
    value = own_ref[:, mine, :]
    for peer in others:
        arrived(landed.at[peer], recv.at[peer])
        value = value + landed[peer]
    part[...] = value
    out_ref[:, mine, :] = value
    for k, peer in enumerate(others):
        copy = push(part, out_ref.at[:, mine, :], gsend.at[k], grecv.at[me], peer, "dp")
        copy.start()
        copies.append(copy)
    for peer in others:
        rows = out_ref.at[:, pl.ds(pl.multiple_of(peer * 16, 16), 16), :]
        arrived(rows, grecv.at[peer])
    for copy in copies:
        copy.wait_send()


def total(own):
    return pl.pallas_call(
        total_kernel,
        out_shape=jax.ShapeDtypeStruct((20, BLOCK, BLOCK), F32),
        in_specs=[VMEM],
        out_specs=VMEM,
        scratch_shapes=[
            pltpu.VMEM((8, 20, 16, BLOCK), F32), pltpu.VMEM((20, 16, BLOCK), F32),
            DMA((8,)), DMA((8,)), DMA((8,)), DMA((8,)),
        ],
        compiler_params=params_of(2),
    )(own)


def pull_many(inverse, matrix_grad):
    highest = lax.Precision.HIGHEST
    left = jnp.einsum("nji,njk->nik", inverse, matrix_grad, precision=highest)
    full = jnp.einsum("nik,njk->nij", left, inverse, precision=highest)
    return -2.0 * (full - full.transpose(0, 2, 1))


def body(tokens, frozen, local_param, cross_param, out_grad):
    gathered = lax.all_gather(out_grad, "tensor", axis=1, tiled=True)
    params = jnp.concatenate([local_param, cross_param.reshape(-1, BLOCK, BLOCK)])
    x, cat, inverse, mats, saved, act = start(tokens, frozen, params)
    output, own = finish(act, frozen, cat, gathered, x, saved, mats)
    matrix_grad = total(own)
    matrix_grad = jnp.concatenate([matrix_grad[:4].transpose(0, 2, 1), matrix_grad[4:]])
    grads = pull_many(inverse, matrix_grad)
    return output, grads[:4], grads[4:].reshape(4, 4, BLOCK, BLOCK)


def solution(mesh):
    in_specs = (
        P("dp", "tensor"),
        P("tensor", None),
        P("tensor", None, None),
        P(None, "tensor", None, None),
        P("dp", "tensor"),
    )
    out_specs = (P("dp", "tensor"), P("tensor", None, None), P(None, "tensor", None, None))
    return jax.shard_map(body, mesh=mesh, in_specs=in_specs, out_specs=out_specs, check_vma=False)
```

time: 397 us -> 210 us (0.53); the launches traced: 392 us -> 210 us
  Pallas kernels: 308 us -> 178 us
  waiting for transfers between devices: 56.8 us -> 5.31 us
    pallas_call x7 -> x3, Pallas kernels: 308 us -> 178 us  [the longest x1 74.5 us: start(): pl.pallas_call(start_kernel, out_shape=(jax.ShapeDtypeStruct((GROUP, ROWS...]
    psum x1 -> x0, waiting for transfers between devices: 56 us -> none  [body(): matrix_grad = lax.psum(matrix_grad, 'dp')]
    all_gather x1, waiting for transfers between devices: 0.02 us -> 4.63 us  [body(): gathered = lax.all_gather(out_grad, 'tensor', axis=1, tiled=True)]
  transfers between devices with their start and end apart: 2 -> 1, of which waited for: 1 -> 1; matrix products, arithmetic and copies ran while one was open for 0% -> 1% of each run, Pallas kernels for 67% -> 36%
where the time goes in v3:
time: 210 us
  Pallas kernels  178 us (85%)
  between operations  14.1 us (7%)
  waiting for transfers between devices  5.31 us (3%)
  matrix products  5.11 us (2%)
  local copies, waits for them, and re-layouts  4.86 us (2%)
  other arithmetic  2.61 us (1%)
    pallas_call x1, Pallas kernels, start(): pl.pallas_call(start_kernel, out_shape=(jax.ShapeDtypeStruct((GROUP, ROWS...  74.5 us
    pallas_call x1, Pallas kernels, finish(): pl.pallas_call(finish_kernel, out_shape=(jax.ShapeDtypeStruct((512, 512),...  60 us
    pallas_call x1, Pallas kernels, total(): pl.pallas_call(total_kernel, out_shape=jax.ShapeDtypeStruct((20, BLOCK, B...  43.3 us
    all_gather x1, waiting for transfers between devices, body(): gathered = lax.all_gather(out_grad, 'tensor', axis=1, tiled=True)  4.63 us
  transfers between devices with their start and end apart: 1, of which 1 were waited for; matrix products, arithmetic and copies ran while one was open for 1% of the time, Pallas kernels for 36%

profile of v3, /device:TPU:6, one launch (start us, length us, event | category | flops | bytes accessed | tf_op | source)
XLA Modules:
  0.0 209.9 jit_solution(2776730780026237318)
XLA Ops:
  7.2 0.0 all-gather.2.cloned.1.call-start
  7.2 0.7 all-gather.2.cloned.1.call-update
  7.9 2.5 %pad_maximum_fusion.param_ref = f32[20,128,128]{2,1,0:T(8,128)} fusion(f32[16,128,128]{2,1,0:T(8,128)} %bitcast.13, f32[4,128,128]{2,1,0:T(8,128)} %param.7), kind=kLoop, calls=%fused_computation | loop fusion | flops 327680 | bytes 2621440 | tf_op jit(solution)/shard_map/concatenate | solution.py:621
  10.4 74.5 %shard_map.76 = (bf16[16,256,128]{2,1,0:T(8,128)(2,1)}, bf16[8,64,4096]{2,1,0:T(8,128)(2,1)}, f32[20,128,128]{2,1,0:T(8,128)}, bf16[4,4,2,256,256]{4,3,2,1,0:T(8...) custom-call(bf16[512,512]{1,0:T(8,128)(2,1)} %tok_ref.1, bf16[8,64,8192]{2,1,0:T(8,128)(2,1)} %bitcast.11, ...), custom_call_target="tpu_custom_call" | custom-call | tf_op jit(solution)/shard_map/pallas_call | solution.py:325
  84.9 4.6 %all-gather.2.cloned.1.call-done.grad_ref = bf16[512,8192]{1,0:T(8,128)(2,1)} async-done(((bf16[512,512]{1,0:T(8,128)(2,1)}), bf16[512,8192]{1,0:T(8,128)(2,1)}) %all-gather.2.cloned.1.call-update) | async-done | bytes 8388624 | tf_op jit(solution)/shard_map/all_gather | solution.py:620
  89.5 60.0 %shard_map.77 = (f32[512,512]{1,0:T(8,128)}, f32[20,128,128]{2,1,0:T(8,128)}) custom-call(bf16[512,1024]{1,0:T(8,128)(2,1)} %get-tuple-element.11.act_hbm, bf16[8,64,8192]{2,1,0:T(8,128)(2,1)} %bitcast.12, bf16[8,64,4096]{2,1,0:T(8,128)(2,1)} %get-tuple-element.12.cat_ref, bf16[512,8192]{1,0:T(8,128)(2,1)} %all-gather.2.cloned.1.call-done.grad_ref, ...), custom_call_target="tpu_custom_call" | custom-call | tf_op jit(solution)/shard_map/pallas_call | solution.py:546
  149.6 43.3 %shard_map.78 = f32[20,128,128]{2,1,0:T(8,128)} custom-call(f32[20,128,128]{2,1,0:T(8,128)} %get-tuple-element.18.own_ref), custom_call_target="tpu_custom_call" | custom-call | tf_op jit(solution)/shard_map/pallas_call | solution.py:599
  192.9 0.0 slice-start
  192.9 0.0 slice-start.1
  192.9 0.0 copy-start
  192.9 0.9 slice-done
  193.8 0.1 copy.10
  193.9 0.2 slice-done.1
  194.2 0.4 copy-done
  194.6 2.3 %fusion = f32[20,128,128]{2,1,0:T(8,128)S(1)} fusion(f32[20,128,128]{2,1,0:T(8,128)S(1)} %copy-done, f32[16,128,128]{2,1,0:T(8,128)S(1)} %slice-done.1, f32[4,128,128]{2,1,0:T(8,128)S(1)} %bitcast.15), kind=kOutput, calls=%fused_computation.1 | convolution fusion | flops 503644160 | bytes 3932160 | tf_op jit(solution)/shard_map/nji,njk->nik/dot_general | solution.py:614
  196.9 2.8 %fusion.6 = f32[20,128,128]{2,1,0:T(8,128)S(1)} fusion(f32[20,128,128]{2,1,0:T(8,128)S(1)} %fusion, f32[20,128,128]{2,1,0:T(8,128)S(1)} %copy-done), kind=kOutput, calls=%fused_computation.8 | convolution fusion | flops 503316480 | bytes 3932160 | tf_op jit(solution)/shard_map/nik,njk->nij/dot_general | solution.py:615
  199.7 0.4 copy.9
  200.1 0.2 fusion.4
  200.3 0.0 copy-start.1
  200.3 0.7 slice.16
  201.0 1.1 slice.17
  202.1 0.0 copy-done.1
  202.1 1.0 copy.12
Async XLA Ops:
  7.2 82.4 %all-gather.2.cloned.1.call-start = ((), (), s32[]{:S(2)}) async-start(), calls=%async_computation | async-start | bytes 8912896 | tf_op jit(solution)/shard_map/all_gather | solution.py:620
  192.9 1.0 slice-start
  192.9 1.3 slice-start.1
  192.9 1.7 copy-start
  200.3 1.8 copy-start.1
Sparse Core Ops, SparseCore 0:
  9.7 79.8 all-gather.1

commit v4 on v3

v4 whole, which is shorter than its diff:
```python
import functools

import jax
import jax.numpy as jnp
from jax import lax
from jax.experimental import pallas as pl
from jax.experimental.pallas import tpu as pltpu
from jax.sharding import PartitionSpec as P

MESH = pl.DeviceIdType.MESH
F32 = jnp.float32
BF16 = jnp.bfloat16
ANY = pl.BlockSpec(memory_space=pl.ANY)
VMEM = pl.BlockSpec(memory_space=pltpu.VMEM)
DMA = pltpu.SemaphoreType.DMA
GROUP = 16
CHIPS = 8
HALF = 64
BLOCK = 128
ROWS = 256


def params_of(identity, vmem=60):
    return pltpu.CompilerParams(
        collective_id=identity, has_side_effects=True, vmem_limit_bytes=vmem << 20
    )


def meet(peers, axis="tensor"):
    barrier = pltpu.get_barrier_semaphore()
    for peer in peers:
        pl.semaphore_signal(barrier, inc=1, device_id={axis: peer}, device_id_type=MESH)
    pl.semaphore_wait(barrier, len(peers))


def push(src, dst, send, recv, peer, axis="tensor"):
    return pltpu.make_async_remote_copy(
        src_ref=src, dst_ref=dst, send_sem=send, recv_sem=recv,
        device_id={axis: peer}, device_id_type=MESH,
    )


def start_job(src, dst, send, recv, peer, me):
    @pl.when(peer == me)
    def _():
        pltpu.make_async_copy(src, dst, recv).start()

    @pl.when(peer != me)
    def _():
        push(src, dst, send, recv, peer).start()


def drain_job(src, dst, send, recv, peer, me):
    @pl.when(peer != me)
    def _():
        push(src, dst, send, recv, peer).wait_send()


def arrived(ref, sem):
    pltpu.make_async_copy(ref, ref, sem).wait()


def split(value):
    high = value.astype(BF16)
    return high, (value - high.astype(F32)).astype(BF16)


def dot(a, b, dims=(((1,), (0,)), ((), ()))):
    return lax.dot_general(a, b, dims, preferred_element_type=F32)


NT = (((1,), (1,)), ((), ()))
TN = (((0,), (0,)), ((), ()))


def dot3(a, b, dims=(((1,), (0,)), ((), ()))):
    return dot(a[0], b[0], dims) + (dot(a[0], b[1], dims) + dot(a[1], b[0], dims))


def inverse_blocks(local_param, cross_param, out_ref, rot_ref):
    count, size, _ = out_ref.shape
    step = 32
    rows = lax.broadcasted_iota(jnp.int32, (size, size), 0)
    lanes = lax.broadcasted_iota(jnp.int32, (size, size), 1)
    panel_rows = lax.broadcasted_iota(jnp.int32, (step, size), 0)
    panel_lanes = lax.broadcasted_iota(jnp.int32, (step, size), 1)
    identity = jnp.where(rows == lanes, 1.0, 0.0)
    for at in range(count):
        param = local_param[at] if at < 4 else cross_param[(at - 4) // 4, at % 4]
        out_ref[at] = identity + param - param.T

    def eliminate(block_at, carry):
        start = pl.multiple_of(block_at * step, step)
        shift = lax.rem(size - start, size)
        inside = (lanes >= start) & (lanes < start + step)
        panels = [pltpu.roll(out_ref[at, pl.ds(start, step), :], shift, 1) for at in range(count)]
        for k in range(step):
            for at in range(count):
                panel = panels[at]
                column = panel[:, k:k + 1]
                scale = 1.0 / panel[k:k + 1, k:k + 1]
                row = jnp.where(panel_lanes[:1] == k, 1.0, panel[k:k + 1, :]) * scale
                rest = jnp.where(panel_lanes == k, 0.0, panel) - column * row
                panels[at] = jnp.where(panel_rows == k, row, rest)
        panels = [pltpu.roll(panel, start, 1) for panel in panels]
        for at in range(count):
            matrix = out_ref[at]
            turned = pltpu.roll(matrix, shift, 1)[:, :step]
            out_ref[at] = jnp.where(inside, 0.0, matrix) - jnp.dot(
                turned, panels[at], precision=lax.Precision.HIGHEST, preferred_element_type=F32
            )
        for at in range(count):
            out_ref[at, pl.ds(start, step), :] = panels[at]
        return carry

    lax.fori_loop(0, size // step, eliminate, 0)
    for at in range(count):
        rotation = 2.0 * out_ref[at] - identity
        rot_ref[at] = rotation.T if at < 4 else rotation


def pair_place(me, level):
    low = 2 ** level
    bit = lax.rem(me // low, 2)
    pair = (me // (2 * low)) * low + lax.rem(me, low)
    return bit, pair


def pair_owner(pair, level, bit):
    low = 2 ** level
    return (pair // low) * (2 * low) + bit * low + lax.rem(pair, low)


def mix(a, b, r):
    at = (r // 2) * BLOCK
    first, second = a[:, at:at + BLOCK], b[:, at:at + BLOCK]
    lanes = lax.broadcasted_iota(jnp.int32, first.shape, 1)
    if r % 2 == 0:
        return jnp.where(lanes < HALF, first, pltpu.roll(second, HALF, 1))
    return jnp.where(lanes < HALF, pltpu.roll(first, HALF, 1), second)


def regroup(quads):
    return [
        jnp.concatenate([mix(quads[0], quads[1], r), mix(quads[2], quads[3], r)], axis=1)
        for r in range(4)
    ]


def place_near(a, b):
    zero = jnp.zeros((BLOCK, BLOCK), F32)
    return jnp.concatenate(
        [jnp.concatenate([a, zero], axis=1), jnp.concatenate([zero, b], axis=1)], axis=0
    )


def place_far(a, b):
    lanes = lax.broadcasted_iota(jnp.int32, (BLOCK, BLOCK), 1)
    turned_a, turned_b = pltpu.roll(a, HALF, 1), pltpu.roll(b, HALF, 1)
    low = lanes < HALF
    a_rows = jnp.concatenate([jnp.where(low, a, 0.0), jnp.where(low, turned_a, 0.0)], axis=1)
    b_rows = jnp.concatenate([jnp.where(low, 0.0, turned_b), jnp.where(low, 0.0, b)], axis=1)
    return jnp.concatenate(
        [a_rows[:HALF], b_rows[:HALF], a_rows[HALF:], b_rows[HALF:]], axis=0
    )


def take_far(full):
    lanes = lax.broadcasted_iota(jnp.int32, (BLOCK, BLOCK), 1)
    low = lanes < HALF
    a_rows = jnp.concatenate([full[:HALF], full[BLOCK:BLOCK + HALF]], axis=0)
    b_rows = jnp.concatenate([full[HALF:BLOCK], full[BLOCK + HALF:]], axis=0)
    a = jnp.where(low, a_rows[:, :BLOCK], pltpu.roll(a_rows[:, BLOCK:], HALF, 1))
    b = jnp.where(low, pltpu.roll(b_rows[:, :BLOCK], HALF, 1), b_rows[:, BLOCK:])
    return a, b


def pairs_of(level, index):
    if level < 2:
        return 2 * index, 2 * index + 1
    return index, 4 + index


ORDER = [(1, 1), (3, 1), (2, 1), (2, 0), (1, 0), (3, 0), (0, 1), (0, 0)]


def layer_kernel(
    tok_ref, froz_ref, grad_ref, local_param, cross_param,
    out_ref, own_ref, inv_ref,
    x_scr, rot, cross, local, mats, saved, rotated, act, weights, grads, sends_buf, lands,
    mine, theirs, landed, rounded, rg, grad_cross, grad_local, cross_in, local_in,
    tsend, trecv, fsend, frecv, wsem, send, recv, lsend, lrecv, psend, precv, asend, arecv,
    gsend, grecv, osend, orecv, rsend, rrecv, bsend, brecv, msend, mrecv, nsend, nrecv,
):
    me = lax.axis_index("tensor")
    core = lax.rem(me, 2)
    chip = me // 2
    partner = me + 1 - 2 * core
    x_at, y_at = lax.rem(chip, 2), chip // 2
    across = 2 * (chip + 1 - 2 * x_at) + core
    up = 2 * lax.rem(chip + 2, CHIPS) + core
    down = 2 * lax.rem(chip + 6, CHIPS) + core
    others = [lax.rem(me + k, GROUP) for k in range(1, GROUP)]
    peers = [lax.rem(me + 2 * k, GROUP) for k in range(1, CHIPS)]
    row = pl.multiple_of(core * ROWS, ROWS)
    other_row = pl.multiple_of((1 - core) * ROWS, ROWS)
    column = pl.multiple_of(chip * BLOCK, BLOCK)
    sends = []

    def go(copy):
        copy.start()
        sends.append(copy)

    def place(dy, dx):
        return ORDER.index((dy, dx))

    def gather(src, slot, half, peer):
        part = src if half is None else src.at[pl.ds(half * ROWS, ROWS), :]
        dst = grads.at[slot] if half is None else grads.at[slot, pl.ds(half * ROWS, ROWS), :]
        at = len(ORDER) if half == 1 else slot
        go(push(part, dst, gsend.at[at], grecv.at[at], peer))

    def gathered(slot, half=None):
        dst = grads.at[slot] if half is None else grads.at[slot, pl.ds(half * ROWS, ROWS), :]
        arrived(dst, grecv.at[len(ORDER) if half == 1 else slot])

    pltpu.make_async_copy(grad_ref, grads.at[place(0, 0)], grecv.at[place(0, 0)]).start()
    fetches = []
    for k, (dy, dx) in enumerate(ORDER):
        target = 2 * lax.rem(y_at + dy, 4) + lax.rem(x_at + dx, 2)
        at = pl.multiple_of((2 * target + core) * 512, 512)
        copy = pltpu.make_async_copy(
            froz_ref.at[:, :, pl.ds(at, 512)], weights.at[k, :, core], wsem.at[k]
        )
        copy.start()
        fetches.append(copy)
    meet(others)

    def token_slice(peer):
        at = pl.multiple_of((peer // 4) * BLOCK, BLOCK)
        start_row = pl.multiple_of(lax.rem(peer, 2) * ROWS, ROWS)
        return tok_ref.at[pl.ds(start_row, ROWS), pl.ds(at, BLOCK)]

    gather(grad_ref, place(3, 0), None, up)
    gather(grad_ref, place(1, 0), None, down)
    gather(grad_ref, place(0, 1), None, across)
    for k, peer in enumerate(others):
        go(push(token_slice(peer), x_scr.at[me], tsend.at[k], trecv.at[me], peer))
    pltpu.make_async_copy(token_slice(me), x_scr.at[me], trecv.at[me]).start()
    for k, (dy, dx) in enumerate(ORDER):
        target = 2 * lax.rem(y_at + dy, 4) + lax.rem(x_at + dx, 2)
        at = pl.multiple_of((2 * target + 1 - core) * 512, 512)
        go(push(
            froz_ref.at[:, :, pl.ds(at, 512)], weights.at[k, :, core], fsend.at[k], frecv.at[k], partner
        ))

    inverse_blocks(local_param, cross_param, inv_ref, rot)

    jobs = []
    for k in range(4):
        c = lax.rem(chip + k, 4)
        for side in range(2):
            jobs.append((
                rot.at[c, pl.ds(side * HALF, HALF), :], local.at[chip, core],
                lsend.at[k, side], lrecv.at[chip], 2 * (2 * c + side) + core, me,
            ))
    for level in range(4):
        bit, pair = pair_place(me, level)
        for k in range(4):
            c = lax.rem(chip + k, 4)
            jobs.append((
                rot.at[4 + 4 * level + c], cross.at[level, pair // 2, lax.rem(pair, 2)],
                send.at[level, k], recv.at[level, pair // 2],
                2 * (c + 4 * bit) + lax.rem(pair, 2), me,
            ))
    for job in jobs:
        start_job(*job)
    gathered(place(0, 1))
    gather(grads.at[place(0, 1)], place(3, 1), None, up)
    gather(grads.at[place(0, 1)], place(1, 1), None, down)
    gathered(place(3, 0))
    gather(grads.at[place(3, 0)], place(2, 0), 0, up)
    gathered(place(1, 0))
    gather(grads.at[place(1, 0)], place(2, 0), 1, down)

    def forward_on(stage):
        if stage == 0:
            for q in range(CHIPS):
                arrived(local.at[q, core], lrecv.at[q])
            part = local.at[:, core]
        else:
            for q in range(4):
                arrived(cross.at[stage - 1, q, core], recv.at[stage - 1, q])
            part = cross.at[stage - 1, :, core]
        go(push(part, part, psend.at[stage], precv.at[stage], partner))

    def weight(k):
        return weights[k].reshape(1024, 512)

    def cotangent(slot, first=False):
        fetches[slot].wait()
        arrived(weights.at[slot, :, 1 - core], frecv.at[slot])
        for rows, total_ref in ((other_row, theirs), (row, mine)):
            value = dot(grads[slot, pl.ds(rows, ROWS), :], weight(slot), NT)
            if first:
                total_ref[...] = value
            else:
                total_ref[...] += value

    forward_on(0)
    forward_on(1)
    for peer in [me] + others:
        arrived(x_scr.at[peer], trecv.at[peer])
    gathered(place(0, 0))
    cotangent(place(0, 0), True)
    arrived(local.at[:, 1 - core], precv.at[0])
    lanes = lax.broadcasted_iota(jnp.int32, (ROWS, BLOCK), 1)
    for m in range(CHIPS):
        parts = []
        for side in range(2):
            high, low = split(jnp.concatenate([local[m, side]] * 2, axis=0))
            x = x_scr[2 * m + side]
            parts.append(dot(x, high, NT) + dot(x, low, NT))
        saved[0, m // 2, :, (m % 2) * BLOCK:(m % 2 + 1) * BLOCK] = jnp.where(
            lanes < HALF, parts[0], parts[1]
        )
    for level in range(4):
        if level < 3:
            forward_on(level + 2)
        if level == 0:
            cotangent(place(0, 1))
            cotangent(place(3, 0))
        if level == 1:
            cotangent(place(1, 0))
        if level == 2:
            gathered(place(2, 0), 0)
            gathered(place(2, 0), 1)
            gather(grads.at[place(2, 0)], place(2, 1), None, across)
            cotangent(place(2, 0))
        arrived(cross.at[level, :, 1 - core], precv.at[level + 1])
        outs = []
        for index in range(4):
            one, two = pairs_of(level, index)
            a = cross[level, one // 2, one % 2]
            b = cross[level, two // 2, two % 2]
            matrix = split(place_near(a, b) if level % 2 == 0 else place_far(a, b))
            mats[level, index, 0] = matrix[0]
            mats[level, index, 1] = matrix[1]
            outs.append(dot3(split(saved[level, index]), matrix))
        if level % 2 == 1:
            outs = regroup(outs)
        for index in range(4):
            if level < 3:
                saved[level + 1, index] = outs[index]
            else:
                rotated[:, index * 256:(index + 1) * 256] = outs[index].astype(BF16)
    landing = act.at[pl.ds(row, ROWS), pl.ds(column, BLOCK)]
    for k, peer in enumerate(peers):
        source = pl.multiple_of((peer // 2) * BLOCK, BLOCK)
        go(push(rotated.at[:, pl.ds(source, BLOCK)], landing, asend.at[k], arecv.at[chip], peer))
    pltpu.make_async_copy(rotated.at[:, pl.ds(column, BLOCK)], landing, arecv.at[chip]).start()
    for slot in (place(3, 1), place(1, 1), place(2, 1)):
        gathered(slot)
        cotangent(slot)
    swap = push(theirs, landed, psend.at[5], precv.at[5], partner)
    swap.start()
    for peer in [me] + peers:
        at = pl.multiple_of((peer // 2) * BLOCK, BLOCK)
        arrived(act.at[pl.ds(row, ROWS), pl.ds(at, BLOCK)], arecv.at[peer // 2])
    part = act.at[pl.ds(row, ROWS), :]
    go(push(part, part, psend.at[6], precv.at[6], partner))
    swap.wait()
    rounded[...] = (mine[...] + landed[...]).astype(BF16)
    landing = rg.at[:, pl.ds(column, BLOCK)]
    for k, peer in enumerate(peers):
        source = pl.multiple_of((peer // 2) * BLOCK, BLOCK)
        go(push(rounded.at[:, pl.ds(source, BLOCK)], landing, rsend.at[k], rrecv.at[chip], peer))
    pltpu.make_async_copy(rounded.at[:, pl.ds(column, BLOCK)], landing, rrecv.at[chip]).start()
    arrived(act.at[pl.ds(other_row, ROWS), :], precv.at[6])

    def product(k, half):
        return dot(act[half * ROWS:(half + 1) * ROWS], weight(k))

    def give(slot, value, peer):
        sends_buf[slot] = value.astype(BF16)
        go(push(sends_buf.at[slot], lands.at[slot], osend.at[slot], orecv.at[slot], peer))

    def take(slot):
        arrived(lands.at[slot], orecv.at[slot])
        return lands[slot].astype(F32)

    for half in range(2):
        for k, peer in ((0, up), (1, down), (2, across)):
            give(2 * k + half, product(k, half), peer)
    give(8, product(4, 1), up)
    give(9, product(5, 0), down)
    for peer in [me] + peers:
        at = pl.multiple_of((peer // 2) * BLOCK, BLOCK)
        arrived(rg.at[:, pl.ds(at, BLOCK)], rrecv.at[peer // 2])

    state = [rg[:, index * 256:(index + 1) * 256].astype(F32) for index in range(4)]
    state = regroup(state)
    swaps = []
    for level in (3, 2, 1, 0):
        outs = []
        for index in range(4):
            grad = split(state[index])
            full = dot3(split(saved[level, index]), grad, TN)
            if level % 2 == 0:
                a, b = full[:BLOCK, :BLOCK], full[BLOCK:, BLOCK:]
            else:
                a, b = take_far(full)
            one, two = pairs_of(level, index)
            grad_cross[level, one % 2, one // 2] = a
            grad_cross[level, two % 2, two // 2] = b
            outs.append(dot3(grad, (mats[level, index, 0], mats[level, index, 1]), NT))
        state = regroup(outs) if level == 2 else outs
        copy = push(
            grad_cross.at[level, 1 - core], cross_in.at[level], bsend.at[level], brecv.at[level], partner
        )
        copy.start()
        swaps.append(copy)
        if level == 3:
            give(6, product(3, 0) + take(4), up)
            give(7, product(3, 1) + take(5), down)
        if level == 1:
            for half in range(2):
                give(12 + half, product(6, half) + (take(0 + half) + take(2 + half)), across)
    for m in range(CHIPS):
        grad = split(state[m // 2][:, (m % 2) * BLOCK:(m % 2 + 1) * BLOCK])
        for side in range(2):
            x = x_scr[2 * m + side]
            full = dot(grad[0], x, TN) + dot(grad[1], x, TN)
            grad_local[side, m] = full[side * HALF:(side + 1) * HALF]
    copy = push(grad_local.at[1 - core], local_in, bsend.at[4], brecv.at[4], partner)
    copy.start()
    swaps.append(copy)
    give(10, product(4, 0) + take(6), up)
    give(11, product(5, 1) + take(7), down)

    for level in (3, 2, 1, 0):
        swaps[3 - level].wait()
        cross_in[level] = cross_in[level] + grad_cross[level, core]
        slot = lax.rem(chip, 4)
        for k in range(4):
            q = lax.rem(chip + k, 4)
            job = (
                cross_in.at[level, q], own_ref.at[4 + 4 * level + slot],
                msend.at[level, k], mrecv.at[level, slot],
                pair_owner(2 * q + core, level, chip // 4), me,
            )
            start_job(*job)
            jobs.append(job)
    swaps[4].wait()
    local_in[...] = local_in[...] + grad_local[core]
    for k in range(CHIPS):
        q = lax.rem(chip + k, CHIPS)
        side = pl.multiple_of(lax.rem(chip, 2) * HALF, HALF)
        job = (
            local_in.at[q], own_ref.at[chip // 2, pl.ds(side, HALF), :],
            nsend.at[k], nrecv.at[chip], 2 * q + core, me,
        )
        start_job(*job)
        jobs.append(job)
    out_ref[0:ROWS] = product(7, 0) + (take(9) + take(12)) + take(10)
    out_ref[ROWS:] = product(7, 1) + (take(8) + take(13)) + take(11)
    for copy in sends:
        copy.wait_send()
    for job in jobs:
        drain_job(*job)
    for level in range(4):
        for c in range(4):
            arrived(own_ref.at[4 + 4 * level + c], mrecv.at[level, c])
    for g in range(CHIPS):
        arrived(own_ref.at[g // 2, pl.ds((g % 2) * HALF, HALF), :], nrecv.at[g])


def layer(tokens, frozen, grads, local_param, cross_param):
    return pl.pallas_call(
        layer_kernel,
        out_shape=(
            jax.ShapeDtypeStruct((512, 512), F32), jax.ShapeDtypeStruct((20, BLOCK, BLOCK), F32),
            jax.ShapeDtypeStruct((20, BLOCK, BLOCK), F32),
        ),
        in_specs=[ANY, ANY, ANY, VMEM, VMEM],
        out_specs=(VMEM, ANY, VMEM),
        scratch_shapes=[
            pltpu.VMEM((GROUP, ROWS, BLOCK), BF16), pltpu.VMEM((20, BLOCK, BLOCK), F32),
            pltpu.VMEM((4, 4, 2, BLOCK, BLOCK), F32), pltpu.VMEM((CHIPS, 2, HALF, BLOCK), F32),
            pltpu.VMEM((4, 4, 2, 256, 256), BF16), pltpu.VMEM((4, 4, ROWS, 256), F32),
            pltpu.VMEM((ROWS, 1024), BF16), pltpu.VMEM((512, 1024), BF16),
            pltpu.VMEM((CHIPS, CHIPS, 2, HALF, 512), BF16), pltpu.VMEM((CHIPS, 512, 512), BF16),
            pltpu.VMEM((14, ROWS, 512), BF16), pltpu.VMEM((14, ROWS, 512), BF16),
            pltpu.VMEM((ROWS, 1024), F32), pltpu.VMEM((ROWS, 1024), F32),
            pltpu.VMEM((ROWS, 1024), F32), pltpu.VMEM((ROWS, 1024), BF16),
            pltpu.VMEM((ROWS, 1024), BF16),
            pltpu.VMEM((4, 2, 4, BLOCK, BLOCK), F32), pltpu.VMEM((2, CHIPS, HALF, BLOCK), F32),
            pltpu.VMEM((4, 4, BLOCK, BLOCK), F32), pltpu.VMEM((CHIPS, HALF, BLOCK), F32),
            DMA((GROUP,)), DMA((GROUP,)), DMA((CHIPS,)), DMA((CHIPS,)), DMA((CHIPS,)),
            DMA((4, 4)), DMA((4, 4)), DMA((4, 2)), DMA((CHIPS,)), DMA((7,)), DMA((7,)),
            DMA((CHIPS,)), DMA((CHIPS,)), DMA((9,)), DMA((9,)), DMA((14,)), DMA((14,)),
            DMA((CHIPS,)), DMA((CHIPS,)), DMA((5,)), DMA((5,)), DMA((4, 4)), DMA((4, 4)),
            DMA((CHIPS,)), DMA((CHIPS,)),
        ],
        compiler_params=params_of(0),
    )(tokens, frozen.reshape(CHIPS, HALF, 8192), grads, local_param, cross_param)


def total_kernel(own_ref, out_ref, landed, part, send, recv, gsend, grecv):
    me = lax.axis_index("dp")
    others = [lax.rem(me + k, 8) for k in range(1, 8)]
    meet(others, "dp")
    copies = []
    for k, peer in enumerate(others):
        rows = own_ref.at[:, pl.ds(pl.multiple_of(peer * 16, 16), 16), :]
        copy = push(rows, landed.at[me], send.at[k], recv.at[me], peer, "dp")
        copy.start()
        copies.append(copy)
    mine = pl.ds(pl.multiple_of(me * 16, 16), 16)
    value = own_ref[:, mine, :]
    for peer in others:
        arrived(landed.at[peer], recv.at[peer])
        value = value + landed[peer]
    part[...] = value
    out_ref[:, mine, :] = value
    for k, peer in enumerate(others):
        copy = push(part, out_ref.at[:, mine, :], gsend.at[k], grecv.at[me], peer, "dp")
        copy.start()
        copies.append(copy)
    for peer in others:
        rows = out_ref.at[:, pl.ds(pl.multiple_of(peer * 16, 16), 16), :]
        arrived(rows, grecv.at[peer])
    for copy in copies:
        copy.wait_send()


def total(own):
    return pl.pallas_call(
        total_kernel,
        out_shape=jax.ShapeDtypeStruct((20, BLOCK, BLOCK), F32),
        in_specs=[VMEM],
        out_specs=VMEM,
        scratch_shapes=[
            pltpu.VMEM((8, 20, 16, BLOCK), F32), pltpu.VMEM((20, 16, BLOCK), F32),
            DMA((8,)), DMA((8,)), DMA((8,)), DMA((8,)),
        ],
        compiler_params=params_of(1),
    )(own)


def pull_many(inverse, matrix_grad):
    highest = lax.Precision.HIGHEST
    left = jnp.einsum("nji,njk->nik", inverse, matrix_grad, precision=highest)
    full = jnp.einsum("nik,njk->nij", left, inverse, precision=highest)
    return -2.0 * (full - full.transpose(0, 2, 1))


def body(tokens, frozen, local_param, cross_param, out_grad):
    output, own, inverse = layer(tokens, frozen, out_grad, local_param, cross_param)
    matrix_grad = total(own)
    matrix_grad = jnp.concatenate([matrix_grad[:4].transpose(0, 2, 1), matrix_grad[4:]])
    grads = pull_many(inverse, matrix_grad)
    return output, grads[:4], grads[4:].reshape(4, 4, BLOCK, BLOCK)


def solution(mesh):
    in_specs = (
        P("dp", "tensor"),
        P("tensor", None),
        P("tensor", None, None),
        P(None, "tensor", None, None),
        P("dp", "tensor"),
    )
    out_specs = (P("dp", "tensor"), P("tensor", None, None), P(None, "tensor", None, None))
    return jax.shard_map(body, mesh=mesh, in_specs=in_specs, out_specs=out_specs, check_vma=False)
```

time: 210 us -> 192 us (0.914)
  between operations: 14.1 us -> 0.71 us
  waiting for transfers between devices: 5.31 us -> 0 us
  Pallas kernels: 178 us -> 181 us
  other arithmetic: 2.61 us -> 0.15 us
    all_gather x1 -> x0, waiting for transfers between devices: 4.63 us -> none  [body(): gathered = lax.all_gather(out_grad, 'tensor', axis=1, tiled=True)]
    pallas_call x2 -> x1, Pallas kernels: 135 us -> 138 us  [layer(): pl.pallas_call(layer_kernel, out_shape=(jax.ShapeDtypeStruct((512, 512),...]
    concatenate x1 -> x0, other arithmetic: 2.46 us -> none  [body(): jnp.concatenate([local_param, cross_param.reshape(-1, BLOCK, BLOCK)])]
  transfers between devices with their start and end apart: 1 -> 0, of which waited for: 1 -> 0; matrix products, arithmetic and copies ran while one was open for 1% -> 0% of each run, Pallas kernels for 36% -> 0%
where the time goes in v4:
time: 192 us
  Pallas kernels  181 us (94%)
  matrix products  5.11 us (3%)
  local copies, waits for them, and re-layouts  4.86 us (3%)
    pallas_call x1, Pallas kernels, layer(): pl.pallas_call(layer_kernel, out_shape=(jax.ShapeDtypeStruct((512, 512),...  138 us
    pallas_call x1, Pallas kernels, total(): pl.pallas_call(total_kernel, out_shape=jax.ShapeDtypeStruct((20, BLOCK, B...  43.7 us

profile of v4, /device:TPU:6, one launch (start us, length us, event | category | flops | bytes accessed | tf_op | source)
XLA Modules:
  0.0 192.1 jit_solution(2810244888344012047)
XLA Ops:
  0.6 137.6 %shard_map.76 = (f32[512,512]{1,0:T(8,128)}, f32[20,128,128]{2,1,0:T(8,128)}, f32[20,128,128]{2,1,0:T(8,128)}) custom-call(bf16[512,512]{1,0:T(8,128)(2,1)} %tok_ref.1, bf16[8,64,8192]{2,1,0:T(8,128)(2,1)} %bitcast.10, bf16[512,512]{1,0:T(8,128)(2,1)} %grad_ref.1, f32[4,128,128]{2,1,0:T(8,128)} %local_param.1, f32[4,4,128,128]{3,2,1,0:T(8,128)} %cross_param.1), custom_call_target="tpu_custom_call" | custom-call | tf_op jit(solution)/shard_map/pallas_call | solution.py:479
  138.2 43.7 %shard_map.77 = f32[20,128,128]{2,1,0:T(8,128)} custom-call(f32[20,128,128]{2,1,0:T(8,128)} %get-tuple-element.8.own_ref), custom_call_target="tpu_custom_call" | custom-call | tf_op jit(solution)/shard_map/pallas_call | solution.py:538
  181.9 0.0 slice-start
  181.9 0.0 slice-start.1
  181.9 0.0 copy-start
  182.0 0.9 slice-done
  182.9 0.1 copy.10
  183.0 0.2 slice-done.1
  183.2 0.4 copy-done
  183.7 2.3 %fusion = f32[20,128,128]{2,1,0:T(8,128)S(1)} fusion(f32[20,128,128]{2,1,0:T(8,128)S(1)} %copy-done, f32[16,128,128]{2,1,0:T(8,128)S(1)} %slice-done.1, f32[4,128,128]{2,1,0:T(8,128)S(1)} %bitcast.12), kind=kOutput, calls=%fused_computation | convolution fusion | flops 503644160 | bytes 3932160 | tf_op jit(solution)/shard_map/nji,njk->nik/dot_general | solution.py:553
  185.9 2.8 %fusion.6 = f32[20,128,128]{2,1,0:T(8,128)S(1)} fusion(f32[20,128,128]{2,1,0:T(8,128)S(1)} %fusion, f32[20,128,128]{2,1,0:T(8,128)S(1)} %copy-done), kind=kOutput, calls=%fused_computation.7 | convolution fusion | flops 503316480 | bytes 3932160 | tf_op jit(solution)/shard_map/nik,njk->nij/dot_general | solution.py:554
  188.8 0.4 copy.9
  189.2 0.2 fusion.4
  189.3 0.0 copy-start.1
  189.3 0.7 slice.16
  190.1 1.1 slice.17
  191.1 0.0 copy-done.1
  191.1 1.0 copy.12
Async XLA Ops:
  181.9 1.0 slice-start
  181.9 1.3 slice-start.1
  181.9 1.7 copy-start
  189.3 1.8 copy-start.1

commit v5 on v4

--- a/solution.py
+++ b/solution.py
@@ -1,5 +1,3 @@
-import functools
-
 import jax
 import jax.numpy as jnp
 from jax import lax
@@ -26,11 +24,13 @@
     )
 
 
-def meet(peers, axis="tensor"):
+def meet(peers, groups):
     barrier = pltpu.get_barrier_semaphore()
     for peer in peers:
-        pl.semaphore_signal(barrier, inc=1, device_id={axis: peer}, device_id_type=MESH)
-    pl.semaphore_wait(barrier, len(peers))
+        pl.semaphore_signal(barrier, inc=1, device_id={"tensor": peer}, device_id_type=MESH)
+    for group in groups:
+        pl.semaphore_signal(barrier, inc=1, device_id={"dp": group}, device_id_type=MESH)
+    pl.semaphore_wait(barrier, len(peers) + len(groups))
 
 
 def push(src, dst, send, recv, peer, axis="tensor"):
@@ -186,11 +186,12 @@
 
 def layer_kernel(
     tok_ref, froz_ref, grad_ref, local_param, cross_param,
-    out_ref, own_ref, inv_ref,
+    out_ref, local_out, cross_out,
     x_scr, rot, cross, local, mats, saved, rotated, act, weights, grads, sends_buf, lands,
     mine, theirs, landed, rounded, rg, grad_cross, grad_local, cross_in, local_in,
+    total_ref, inv_ref, own, z_send, z_land, z_sum, side_land,
     tsend, trecv, fsend, frecv, wsem, send, recv, lsend, lrecv, psend, precv, asend, arecv,
-    gsend, grecv, osend, orecv, rsend, rrecv, bsend, brecv, msend, mrecv, nsend, nrecv,
+    gsend, grecv, osend, orecv, rsend, rrecv, bsend, brecv, msend, mrecv, nsend, nrecv, zsend, zrecv,
 ):
     me = lax.axis_index("tensor")
     core = lax.rem(me, 2)
@@ -234,7 +235,11 @@
         )
         copy.start()
         fetches.append(copy)
-    meet(others)
+    batch = lax.axis_index("dp")
+    z_at, side_at = batch // 2, lax.rem(batch, 2)
+    z_peers = [lax.rem(z_at + k, 4) for k in range(1, 4)]
+    side_peer = 2 * z_at + 1 - side_at
+    meet(others, [2 * z + side_at for z in z_peers] + [side_peer])
 
     def token_slice(peer):
         at = pl.multiple_of((peer // 4) * BLOCK, BLOCK)
@@ -273,15 +278,15 @@
                 send.at[level, k], recv.at[level, pair // 2],
                 2 * (c + 4 * bit) + lax.rem(pair, 2), me,
             ))
+    gathered(place(3, 0))
+    gather(grads.at[place(3, 0)], place(2, 0), 0, up)
+    gathered(place(1, 0))
+    gather(grads.at[place(1, 0)], place(2, 0), 1, down)
     for job in jobs:
         start_job(*job)
     gathered(place(0, 1))
     gather(grads.at[place(0, 1)], place(3, 1), None, up)
     gather(grads.at[place(0, 1)], place(1, 1), None, down)
-    gathered(place(3, 0))
-    gather(grads.at[place(3, 0)], place(2, 0), 0, up)
-    gathered(place(1, 0))
-    gather(grads.at[place(1, 0)], place(2, 0), 1, down)
 
     def forward_on(stage):
         if stage == 0:
@@ -328,14 +333,14 @@
         if level < 3:
             forward_on(level + 2)
         if level == 0:
+            gathered(place(2, 0), 0)
+            gathered(place(2, 0), 1)
+            gather(grads.at[place(2, 0)], place(2, 1), None, across)
             cotangent(place(0, 1))
             cotangent(place(3, 0))
         if level == 1:
             cotangent(place(1, 0))
         if level == 2:
-            gathered(place(2, 0), 0)
-            gathered(place(2, 0), 1)
-            gather(grads.at[place(2, 0)], place(2, 1), None, across)
             cotangent(place(2, 0))
         arrived(cross.at[level, :, 1 - core], precv.at[level + 1])
         outs = []
@@ -381,19 +386,17 @@
     def product(k, half):
         return dot(act[half * ROWS:(half + 1) * ROWS], weight(k))
 
+    def ready(slot, value):
+        sends_buf[slot] = value.astype(BF16)
+
     def give(slot, value, peer):
-        sends_buf[slot] = value.astype(BF16)
+        ready(slot, value)
         go(push(sends_buf.at[slot], lands.at[slot], osend.at[slot], orecv.at[slot], peer))
 
     def take(slot):
         arrived(lands.at[slot], orecv.at[slot])
         return lands[slot].astype(F32)
 
-    for half in range(2):
-        for k, peer in ((0, up), (1, down), (2, across)):
-            give(2 * k + half, product(k, half), peer)
-    give(8, product(4, 1), up)
-    give(9, product(5, 0), down)
     for peer in [me] + peers:
         at = pl.multiple_of((peer // 2) * BLOCK, BLOCK)
         arrived(rg.at[:, pl.ds(at, BLOCK)], rrecv.at[peer // 2])
@@ -420,12 +423,6 @@
         )
         copy.start()
         swaps.append(copy)
-        if level == 3:
-            give(6, product(3, 0) + take(4), up)
-            give(7, product(3, 1) + take(5), down)
-        if level == 1:
-            for half in range(2):
-                give(12 + half, product(6, half) + (take(0 + half) + take(2 + half)), across)
     for m in range(CHIPS):
         grad = split(state[m // 2][:, (m % 2) * BLOCK:(m % 2 + 1) * BLOCK])
         for side in range(2):
@@ -435,9 +432,6 @@
     copy = push(grad_local.at[1 - core], local_in, bsend.at[4], brecv.at[4], partner)
     copy.start()
     swaps.append(copy)
-    give(10, product(4, 0) + take(6), up)
-    give(11, product(5, 1) + take(7), down)
-
     for level in (3, 2, 1, 0):
         swaps[3 - level].wait()
         cross_in[level] = cross_in[level] + grad_cross[level, core]
@@ -445,7 +439,7 @@
         for k in range(4):
             q = lax.rem(chip + k, 4)
             job = (
-                cross_in.at[level, q], own_ref.at[4 + 4 * level + slot],
+                cross_in.at[level, q], own.at[4 + 4 * level + slot],
                 msend.at[level, k], mrecv.at[level, slot],
                 pair_owner(2 * q + core, level, chip // 4), me,
             )
@@ -457,33 +451,82 @@
         q = lax.rem(chip + k, CHIPS)
         side = pl.multiple_of(lax.rem(chip, 2) * HALF, HALF)
         job = (
-            local_in.at[q], own_ref.at[chip // 2, pl.ds(side, HALF), :],
+            local_in.at[q], own.at[chip // 2, pl.ds(side, HALF), :],
             nsend.at[k], nrecv.at[chip], 2 * q + core, me,
         )
         start_job(*job)
         jobs.append(job)
+    for half in range(2):
+        for k in range(3):
+            ready(2 * k + half, product(k, half))
+    for level in range(4):
+        for c in range(4):
+            arrived(own.at[4 + 4 * level + c], mrecv.at[level, c])
+    for g in range(CHIPS):
+        arrived(own.at[g // 2, pl.ds((g % 2) * HALF, HALF), :], nrecv.at[g])
+    own_rows = pl.ds(pl.multiple_of(z_at * 32, 32), 32)
+    for k, z in enumerate(z_peers):
+        z_send[k] = own[:, pl.ds(pl.multiple_of(z * 32, 32), 32), :].astype(BF16)
+        go(push(z_send.at[k], z_land.at[z_at], zsend.at[k], zrecv.at[z_at], 2 * z + side_at, "dp"))
+    for half in range(2):
+        for k, peer in ((0, up), (1, down), (2, across)):
+            slot = 2 * k + half
+            go(push(sends_buf.at[slot], lands.at[slot], osend.at[slot], orecv.at[slot], peer))
+    give(8, product(4, 1), up)
+    give(9, product(5, 0), down)
+    value = own[:, own_rows, :]
+    for z in z_peers:
+        arrived(z_land.at[z], zrecv.at[z])
+        value = value + z_land[z].astype(F32)
+    z_sum[...] = value
+    their_part = pl.ds(pl.multiple_of((1 - side_at) * 16, 16), 16)
+    my_part = pl.ds(pl.multiple_of(side_at * 16, 16), 16)
+    go(push(z_sum.at[:, their_part, :], side_land, zsend.at[3], zrecv.at[4], side_peer, "dp"))
+    give(6, product(3, 0) + take(4), up)
+    give(7, product(3, 1) + take(5), down)
+    for half in range(2):
+        give(12 + half, product(6, half) + (take(0 + half) + take(2 + half)), across)
+    arrived(side_land, zrecv.at[4])
+    my_rows = pl.ds(pl.multiple_of(z_at * 32 + side_at * 16, 16), 16)
+    their_rows = pl.ds(pl.multiple_of(z_at * 32 + (1 - side_at) * 16, 16), 16)
+    total_ref[:, my_rows, :] = z_sum[:, my_part, :] + side_land[...]
+    mine_rows = total_ref.at[:, my_rows, :]
+    go(push(mine_rows, mine_rows, zsend.at[4], zrecv.at[5], side_peer, "dp"))
+    give(10, product(4, 0) + take(6), up)
+    give(11, product(5, 1) + take(7), down)
+    arrived(total_ref.at[:, their_rows, :], zrecv.at[5])
+    both = total_ref.at[:, own_rows, :]
+    for k, z in enumerate(z_peers):
+        go(push(both, both, zsend.at[5 + k], zrecv.at[6 + z_at], 2 * z + side_at, "dp"))
     out_ref[0:ROWS] = product(7, 0) + (take(9) + take(12)) + take(10)
     out_ref[ROWS:] = product(7, 1) + (take(8) + take(13)) + take(11)
+    for z in z_peers:
+        arrived(total_ref.at[:, pl.ds(pl.multiple_of(z * 32, 32), 32), :], zrecv.at[6 + z])
+    for at in range(20):
+        matrix = total_ref[at].T if at < 4 else total_ref[at]
+        inverse = split(inv_ref[at])
+        left = dot3(inverse, split(matrix), TN)
+        full = dot3(split(left), inverse, NT)
+        pulled = -2.0 * (full - full.T)
+        if at < 4:
+            local_out[at] = pulled
+        else:
+            cross_out[(at - 4) // 4, at % 4] = pulled
     for copy in sends:
         copy.wait_send()
     for job in jobs:
         drain_job(*job)
-    for level in range(4):
-        for c in range(4):
-            arrived(own_ref.at[4 + 4 * level + c], mrecv.at[level, c])
-    for g in range(CHIPS):
-        arrived(own_ref.at[g // 2, pl.ds((g % 2) * HALF, HALF), :], nrecv.at[g])
 
 
 def layer(tokens, frozen, grads, local_param, cross_param):
     return pl.pallas_call(
         layer_kernel,
         out_shape=(
-            jax.ShapeDtypeStruct((512, 512), F32), jax.ShapeDtypeStruct((20, BLOCK, BLOCK), F32),
-            jax.ShapeDtypeStruct((20, BLOCK, BLOCK), F32),
+            jax.ShapeDtypeStruct((512, 512), F32), jax.ShapeDtypeStruct((4, BLOCK, BLOCK), F32),
+            jax.ShapeDtypeStruct((4, 4, BLOCK, BLOCK), F32),
         ),
         in_specs=[ANY, ANY, ANY, VMEM, VMEM],
-        out_specs=(VMEM, ANY, VMEM),
+        out_specs=(VMEM, VMEM, VMEM),
         scratch_shapes=[
             pltpu.VMEM((GROUP, ROWS, BLOCK), BF16), pltpu.VMEM((20, BLOCK, BLOCK), F32),
             pltpu.VMEM((4, 4, 2, BLOCK, BLOCK), F32), pltpu.VMEM((CHIPS, 2, HALF, BLOCK), F32),
@@ -496,71 +539,22 @@
             pltpu.VMEM((ROWS, 1024), BF16),
             pltpu.VMEM((4, 2, 4, BLOCK, BLOCK), F32), pltpu.VMEM((2, CHIPS, HALF, BLOCK), F32),
             pltpu.VMEM((4, 4, BLOCK, BLOCK), F32), pltpu.VMEM((CHIPS, HALF, BLOCK), F32),
+            pltpu.VMEM((20, BLOCK, BLOCK), F32), pltpu.VMEM((20, BLOCK, BLOCK), F32),
+            pltpu.VMEM((20, BLOCK, BLOCK), F32), pltpu.VMEM((3, 20, 32, BLOCK), BF16),
+            pltpu.VMEM((4, 20, 32, BLOCK), BF16), pltpu.VMEM((20, 32, BLOCK), F32),
+            pltpu.VMEM((20, 16, BLOCK), F32),
             DMA((GROUP,)), DMA((GROUP,)), DMA((CHIPS,)), DMA((CHIPS,)), DMA((CHIPS,)),
             DMA((4, 4)), DMA((4, 4)), DMA((4, 2)), DMA((CHIPS,)), DMA((7,)), DMA((7,)),
             DMA((CHIPS,)), DMA((CHIPS,)), DMA((9,)), DMA((9,)), DMA((14,)), DMA((14,)),
             DMA((CHIPS,)), DMA((CHIPS,)), DMA((5,)), DMA((5,)), DMA((4, 4)), DMA((4, 4)),
-            DMA((CHIPS,)), DMA((CHIPS,)),
+            DMA((CHIPS,)), DMA((CHIPS,)), DMA((8,)), DMA((10,)),
         ],
         compiler_params=params_of(0),
     )(tokens, frozen.reshape(CHIPS, HALF, 8192), grads, local_param, cross_param)
 
 
-def total_kernel(own_ref, out_ref, landed, part, send, recv, gsend, grecv):
-    me = lax.axis_index("dp")
-    others = [lax.rem(me + k, 8) for k in range(1, 8)]
-    meet(others, "dp")
-    copies = []
-    for k, peer in enumerate(others):
-        rows = own_ref.at[:, pl.ds(pl.multiple_of(peer * 16, 16), 16), :]
-        copy = push(rows, landed.at[me], send.at[k], recv.at[me], peer, "dp")
-        copy.start()
-        copies.append(copy)
-    mine = pl.ds(pl.multiple_of(me * 16, 16), 16)
-    value = own_ref[:, mine, :]
-    for peer in others:
-        arrived(landed.at[peer], recv.at[peer])
-        value = value + landed[peer]
-    part[...] = value
-    out_ref[:, mine, :] = value
-    for k, peer in enumerate(others):
-        copy = push(part, out_ref.at[:, mine, :], gsend.at[k], grecv.at[me], peer, "dp")
-        copy.start()
-        copies.append(copy)
-    for peer in others:
-        rows = out_ref.at[:, pl.ds(pl.multiple_of(peer * 16, 16), 16), :]
-        arrived(rows, grecv.at[peer])
-    for copy in copies:
-        copy.wait_send()
-
-
-def total(own):
-    return pl.pallas_call(
-        total_kernel,
-        out_shape=jax.ShapeDtypeStruct((20, BLOCK, BLOCK), F32),
-        in_specs=[VMEM],
-        out_specs=VMEM,
-        scratch_shapes=[
-            pltpu.VMEM((8, 20, 16, BLOCK), F32), pltpu.VMEM((20, 16, BLOCK), F32),
-            DMA((8,)), DMA((8,)), DMA((8,)), DMA((8,)),
-        ],
-        compiler_params=params_of(1),
-    )(own)
-
-
-def pull_many(inverse, matrix_grad):
-    highest = lax.Precision.HIGHEST
-    left = jnp.einsum("nji,njk->nik", inverse, matrix_grad, precision=highest)
-    full = jnp.einsum("nik,njk->nij", left, inverse, precision=highest)
-    return -2.0 * (full - full.transpose(0, 2, 1))
-
-
 def body(tokens, frozen, local_param, cross_param, out_grad):
-    output, own, inverse = layer(tokens, frozen, out_grad, local_param, cross_param)
-    matrix_grad = total(own)
-    matrix_grad = jnp.concatenate([matrix_grad[:4].transpose(0, 2, 1), matrix_grad[4:]])
-    grads = pull_many(inverse, matrix_grad)
-    return output, grads[:4], grads[4:].reshape(4, 4, BLOCK, BLOCK)
+    return layer(tokens, frozen, out_grad, local_param, cross_param)
 
 
 def solution(mesh):

time: 192 us -> 166 us (0.86)
  Pallas kernels: 181 us -> 158 us
  matrix products: 5.11 us -> 0 us
    pallas_call x1 -> x0, Pallas kernels: 43.7 us -> none  [total(): pl.pallas_call(total_kernel, out_shape=jax.ShapeDtypeStruct((20, BLOCK, B...]
    pallas_call x1, Pallas kernels: 138 us -> 158 us  [layer(): pl.pallas_call(layer_kernel, out_shape=(jax.ShapeDtypeStruct((512, 512),...]
    dot_general x2 -> x0, matrix products: 5.11 us -> none  [the longest x1 2.84 us: pull_many(): full = jnp.einsum('nik,njk->nij', left, inverse, precision=highest)]
    unnamed x6 -> x3, local copies, waits for them, and re-layouts: 1.52 us -> 6.23 us
    slice x6 -> x0, local copies, waits for them, and re-layouts: 2.94 us -> none  [the longest x2 1.78 us: body(): return (output, grads[:4], grads[4:].reshape(4, 4, BLOCK, BLOCK))]
where the time goes in v5:
time: 166 us; the launch traced here: 165 us
  Pallas kernels  158 us (95%)
  local copies, waits for them, and re-layouts  6.23 us (4%)
    pallas_call x1, Pallas kernels, layer(): pl.pallas_call(layer_kernel, out_shape=(jax.ShapeDtypeStruct((512, 512),...  158 us
    unnamed x3, local copies, waits for them, and re-layouts  6.23 us

profile of v5, /device:TPU:6, one launch (start us, length us, event | category | flops | bytes accessed | tf_op | source)
XLA Modules:
  0.0 165.2 jit_solution(12883412416150730991)
XLA Ops:
  0.6 158.3 %shard_map.76 = (f32[512,512]{1,0:T(8,128)}, f32[4,128,128]{2,1,0:T(8,128)}, f32[4,4,128,128]{3,2,1,0:T(8,128)}) custom-call(bf16[512,512]{1,0:T(8,128)(2,1)} %tok_ref.1, bf16[8,64,8192]{2,1,0:T(8,128)(2,1)} %bitcast.1, bf16[512,512]{1,0:T(8,128)(2,1)} %grad_ref.1, f32[4,128,128]{2,1,0:T(8,128)} %local_param.1, f32[4,4,128,128]{3,2,1,0:T(8,128)} %cross_param.1), custom_call_target="tpu_custom_call" | custom-call | tf_op jit(solution)/shard_map/pallas_call | solution.py:522
  158.9 2.3 %copy.11 = f32[512,512]{1,0:T(8,128)} copy(f32[512,512]{1,0:T(8,128)} %get-tuple-element.6) | data formatting | bytes 2097152
  161.2 1.7 %copy.12 = f32[4,128,128]{2,1,0:T(8,128)} copy(f32[4,128,128]{2,1,0:T(8,128)} %get-tuple-element.7) | data formatting | bytes 524288
  162.9 2.3 %copy.13 = f32[4,4,128,128]{3,2,1,0:T(8,128)} copy(f32[4,4,128,128]{3,2,1,0:T(8,128)} %get-tuple-element.8) | data formatting | bytes 2097152

commit v6 on v5

--- a/solution.py
+++ b/solution.py
@@ -359,21 +359,11 @@
                 saved[level + 1, index] = outs[index]
             else:
                 rotated[:, index * 256:(index + 1) * 256] = outs[index].astype(BF16)
-    landing = act.at[pl.ds(row, ROWS), pl.ds(column, BLOCK)]
-    for k, peer in enumerate(peers):
-        source = pl.multiple_of((peer // 2) * BLOCK, BLOCK)
-        go(push(rotated.at[:, pl.ds(source, BLOCK)], landing, asend.at[k], arecv.at[chip], peer))
-    pltpu.make_async_copy(rotated.at[:, pl.ds(column, BLOCK)], landing, arecv.at[chip]).start()
     for slot in (place(3, 1), place(1, 1), place(2, 1)):
         gathered(slot)
         cotangent(slot)
     swap = push(theirs, landed, psend.at[5], precv.at[5], partner)
     swap.start()
-    for peer in [me] + peers:
-        at = pl.multiple_of((peer // 2) * BLOCK, BLOCK)
-        arrived(act.at[pl.ds(row, ROWS), pl.ds(at, BLOCK)], arecv.at[peer // 2])
-    part = act.at[pl.ds(row, ROWS), :]
-    go(push(part, part, psend.at[6], precv.at[6], partner))
     swap.wait()
     rounded[...] = (mine[...] + landed[...]).astype(BF16)
     landing = rg.at[:, pl.ds(column, BLOCK)]
@@ -381,7 +371,11 @@
         source = pl.multiple_of((peer // 2) * BLOCK, BLOCK)
         go(push(rounded.at[:, pl.ds(source, BLOCK)], landing, rsend.at[k], rrecv.at[chip], peer))
     pltpu.make_async_copy(rounded.at[:, pl.ds(column, BLOCK)], landing, rrecv.at[chip]).start()
-    arrived(act.at[pl.ds(other_row, ROWS), :], precv.at[6])
+    landing = act.at[pl.ds(row, ROWS), pl.ds(column, BLOCK)]
+    for k, peer in enumerate(peers):
+        source = pl.multiple_of((peer // 2) * BLOCK, BLOCK)
+        go(push(rotated.at[:, pl.ds(source, BLOCK)], landing, asend.at[k], arecv.at[chip], peer))
+    pltpu.make_async_copy(rotated.at[:, pl.ds(column, BLOCK)], landing, arecv.at[chip]).start()
 
     def product(k, half):
         return dot(act[half * ROWS:(half + 1) * ROWS], weight(k))
@@ -404,6 +398,21 @@
     state = [rg[:, index * 256:(index + 1) * 256].astype(F32) for index in range(4)]
     state = regroup(state)
     swaps = []
+
+    def send_back(level):
+        swaps[3 - level].wait()
+        cross_in[level] = cross_in[level] + grad_cross[level, core]
+        slot = lax.rem(chip, 4)
+        for k in range(4):
+            q = lax.rem(chip + k, 4)
+            job = (
+                cross_in.at[level, q], own.at[4 + 4 * level + slot],
+                msend.at[level, k], mrecv.at[level, slot],
+                pair_owner(2 * q + core, level, chip // 4), me,
+            )
+            start_job(*job)
+            jobs.append(job)
+
     for level in (3, 2, 1, 0):
         outs = []
         for index in range(4):
@@ -423,6 +432,14 @@
         )
         copy.start()
         swaps.append(copy)
+        if level == 3:
+            for peer in [me] + peers:
+                at = pl.multiple_of((peer // 2) * BLOCK, BLOCK)
+                arrived(act.at[pl.ds(row, ROWS), pl.ds(at, BLOCK)], arecv.at[peer // 2])
+            part = act.at[pl.ds(row, ROWS), :]
+            go(push(part, part, psend.at[6], precv.at[6], partner))
+        else:
+            send_back(level + 1)
     for m in range(CHIPS):
         grad = split(state[m // 2][:, (m % 2) * BLOCK:(m % 2 + 1) * BLOCK])
         for side in range(2):
@@ -432,19 +449,7 @@
     copy = push(grad_local.at[1 - core], local_in, bsend.at[4], brecv.at[4], partner)
     copy.start()
     swaps.append(copy)
-    for level in (3, 2, 1, 0):
-        swaps[3 - level].wait()
-        cross_in[level] = cross_in[level] + grad_cross[level, core]
-        slot = lax.rem(chip, 4)
-        for k in range(4):
-            q = lax.rem(chip + k, 4)
-            job = (
-                cross_in.at[level, q], own.at[4 + 4 * level + slot],
-                msend.at[level, k], mrecv.at[level, slot],
-                pair_owner(2 * q + core, level, chip // 4), me,
-            )
-            start_job(*job)
-            jobs.append(job)
+    send_back(0)
     swaps[4].wait()
     local_in[...] = local_in[...] + grad_local[core]
     for k in range(CHIPS):
@@ -456,6 +461,7 @@
         )
         start_job(*job)
         jobs.append(job)
+    arrived(act.at[pl.ds(other_row, ROWS), :], precv.at[6])
     for half in range(2):
         for k in range(3):
             ready(2 * k + half, product(k, half))

time: 166 us -> 167 us (level)
  the two profiles are of different devices: /device:TPU:6 before, /device:TPU:8 now
where the time goes in v6:
time: 167 us; the launch traced here: 166 us
  Pallas kernels  160 us (96%)
  local copies, waits for them, and re-layouts  6.23 us (4%)
    pallas_call x1, Pallas kernels, layer(): pl.pallas_call(layer_kernel, out_shape=(jax.ShapeDtypeStruct((512, 512),...  160 us
    unnamed x3, local copies, waits for them, and re-layouts  6.23 us

profile of v6, /device:TPU:8, one launch (start us, length us, event | category | flops | bytes accessed | tf_op | source)
XLA Modules:
  0.0 166.4 jit_solution(12860187996286427693)
XLA Ops:
  0.6 159.5 %shard_map.76 = (f32[512,512]{1,0:T(8,128)}, f32[4,128,128]{2,1,0:T(8,128)}, f32[4,4,128,128]{3,2,1,0:T(8,128)}) custom-call(bf16[512,512]{1,0:T(8,128)(2,1)} %tok_ref.1, bf16[8,64,8192]{2,1,0:T(8,128)(2,1)} %bitcast.1, bf16[512,512]{1,0:T(8,128)(2,1)} %grad_ref.1, f32[4,128,128]{2,1,0:T(8,128)} %local_param.1, f32[4,4,128,128]{3,2,1,0:T(8,128)} %cross_param.1), custom_call_target="tpu_custom_call" | custom-call | tf_op jit(solution)/shard_map/pallas_call | solution.py:528
  160.2 2.3 %copy.11 = f32[512,512]{1,0:T(8,128)} copy(f32[512,512]{1,0:T(8,128)} %get-tuple-element.6) | data formatting | bytes 2097152
  162.4 1.7 %copy.12 = f32[4,128,128]{2,1,0:T(8,128)} copy(f32[4,128,128]{2,1,0:T(8,128)} %get-tuple-element.7) | data formatting | bytes 524288
  164.1 2.3 %copy.13 = f32[4,4,128,128]{3,2,1,0:T(8,128)} copy(f32[4,4,128,128]{3,2,1,0:T(8,128)} %get-tuple-element.8) | data formatting | bytes 2097152
